TPU v7x, 32 devices: a whole 2x2x4 slice. The times are simulated.
32 devices in a mesh: tm: 4 (over z), height: 8 (over y, x, core).
Axes of the slice: x: 2, y: 2, z: 4, core: 2. Of those that a mesh axis runs over, the one named last changes fastest.
Arguments:
- queries: bfloat16 [16, 16, 16, 2560], P('tm', 'height'), may hold values from -64 to 64
- keys: bfloat16 [16, 16, 16, 2560], P('tm', 'height'), may hold values from -64 to 64
- values: bfloat16 [16, 16, 16, 2560], P('tm', 'height'), may hold values from -6 to 6
- tile_mask: int32 [4, 8, 2, 18], P('tm', 'height'), may hold values 0 or 1
- sink_frame: int32 [1], replicated, may hold values from 0 to 15
Outputs:
- attended: bfloat16 [16, 16, 16, 2560], P('tm', 'height')
All inputs are finite; a program needn't handle non-finite values. No bound on the sum of `tile_mask` on one device may be relied on, other than what follows from the above.
Results may differ from a plain program's by a relative error of at most 0.0041.
Values may be sent and summed in bfloat16 or wider, within the bound.
No kernel may reach another device: no remote copies, remote signals or barrier semaphores. Data moves between devices by JAX's collectives and lax.ppermute only.
A program may use at most 128 MiB of HBM per device.

v0:
```python
import math

import jax
import jax.numpy as jnp
from jax import lax
from jax.experimental import pallas as pl
from jax.experimental.pallas import tpu as pltpu
from jax.sharding import PartitionSpec as P


HD = 128
TF = 4
TC = 8
CHUNKS = 2
NEG = -1e30
AUX = 128
GRANT = 12 << 20


def split3(x):
    hi = x.astype(jnp.bfloat16).astype(jnp.float32)
    mid = (x - hi).astype(jnp.bfloat16).astype(jnp.float32)
    return hi, mid, x - hi - mid


def dot(x, y, contract):
    dims = (((contract,), (contract,)), ((), ()))
    return lax.dot_general(x, y, dims, preferred_element_type=jnp.float32)


VMEM = pltpu.MemorySpace.VMEM


def near_core(x):
    return pltpu.with_memory_space_constraint(x, VMEM)


def lanes(head):
    return pl.ds(pl.multiple_of(head * HD, HD), HD)


def attend_kernel(chunk, heads, group, scale, places, q_part, own, *refs):
    q, flags = refs[:2]
    n_bands = len(places)
    keys = refs[2 : 2 + n_bands]
    vals = refs[2 + n_bands : 2 + 2 * n_bands]
    acc, stat, bias = refs[2 + 2 * n_bands :]
    tokens = q.shape[0]
    pad = stat.shape[0] // 2

    second = (lax.broadcasted_iota(jnp.int32, (tokens, tokens), 0) // TC) % 2 == 1
    kept = jnp.where(flags[:, flags.shape[1] - AUX :].astype(jnp.float32).T > 0.5, 0.0, NEG)
    for j in range(n_bands):
        one = jnp.broadcast_to(kept[2 * j : 2 * j + 1], second.shape)
        two = jnp.broadcast_to(kept[2 * j + 1 : 2 * j + 2], second.shape)
        bias[j * tokens : (j + 1) * tokens] = jnp.where(second, two, one)
    stat[...] = jnp.zeros_like(stat)

    def step(i, _):
        for g in range(group):
            head = i * group + g
            there = lanes(chunk * heads + head)
            here = lanes(head)
            k = jnp.concatenate(
                [
                    r[row * tokens : (row + 1) * tokens, here if part else there]
                    for r, (row, _, part) in zip(keys, places)
                ],
                axis=0,
            )
            v = jnp.concatenate(
                [
                    r[row * tokens : (row + 1) * tokens, here if part else there]
                    for r, (_, row, part) in zip(vals, places)
                ],
                axis=0,
            )
            s = dot(k, q[:, here if q_part else there], 1) * scale + bias[...]
            m = jnp.max(s, axis=0, keepdims=True)
            p = jnp.exp2(s - m).astype(jnp.bfloat16)
            acc[here] = dot(v, p, 0).astype(acc.dtype)
            stat[pl.ds(head, 1)] = m
            stat[pl.ds(pad + head, 1)] = jnp.sum(p.astype(jnp.float32), axis=0, keepdims=True)
        return 0

    lax.fori_loop(0, heads // group, step, 0)
    if not own:
        parts = split3(stat[:pad]) + split3(stat[pad:])[:2]
        for i, part in enumerate(parts):
            acc[heads * HD + i * pad : heads * HD + (i + 1) * pad] = part.astype(acc.dtype)


def padded(heads):
    return -(-heads // 16) * 16


def attend(chunk, heads, group, scale, q, q_part, flags, bands, own):
    tokens, pad = q.shape[0], padded(heads)
    args = [q, flags] + [b[0] for b in bands] + [b[1] for b in bands]
    places = [b[2:] for b in bands]
    keys = len(bands) * tokens
    stat = (2 * pad, tokens)
    vmem = pl.BlockSpec(memory_space=VMEM)
    if own:
        out_shape = (pltpu.VMEM((heads * HD, tokens), jnp.float32), pltpu.VMEM(stat, jnp.float32))
        scratch = []
    else:
        out_shape = (pltpu.VMEM((heads * HD + 5 * pad, tokens), jnp.bfloat16),)
        scratch = [pltpu.VMEM(stat, jnp.float32)]
    pairs = tokens * keys * heads
    return pl.pallas_call(
        lambda *refs: attend_kernel(chunk, heads, group, scale, places, q_part, own, *refs),
        in_specs=[vmem] * len(args),
        out_specs=(vmem,) * len(out_shape),
        out_shape=out_shape,
        scratch_shapes=scratch + [pltpu.VMEM((keys, tokens), jnp.float32)],
        cost_estimate=pl.CostEstimate(
            flops=6 * pairs * HD, bytes_accessed=10 * tokens * heads * HD * 2, transcendentals=pairs
        ),
        compiler_params=pltpu.CompilerParams(vmem_limit_bytes=GRANT),
        name="attend",
    )(*[near_core(x) for x in args])


def merge_kernel(heads, group, scale, n_sink, *refs):
    q, pieces = refs[0], refs[1 : 1 + n_sink]
    accs, stats, outs = (refs[1 + n_sink + i * CHUNKS :][:CHUNKS] for i in range(3))
    stat = refs[-1]
    rows = pieces[0].shape[0] // 2
    pad = padded(heads)
    stat[...] = jnp.zeros_like(stat)
    for c in range(CHUNKS):

        def step(i, _):
            for g in range(group):
                head = i * group + g
                there, here = lanes(c * heads + head), lanes(head)
                m1, l1 = stats[c][pl.ds(head, 1)], stats[c][pl.ds(pad + head, 1)]
                k = jnp.concatenate([r[:rows, there] for r in pieces], axis=0)
                v = jnp.concatenate([r[rows:, there] for r in pieces], axis=0)
                s = dot(k, q[:, there], 1) * scale
                top = jnp.maximum(jnp.max(s, axis=0, keepdims=True), m1)
                p = jnp.exp2(s - top).astype(jnp.bfloat16)
                f = jnp.exp2(m1 - top)
                outs[c][here] = dot(v, p, 0) + accs[c][here] * f
                total = jnp.sum(p.astype(jnp.float32), axis=0, keepdims=True) + f * l1
                stat[pl.ds(2 * c * pad + head, 1)] = top
                stat[pl.ds((2 * c + 1) * pad + head, 1)] = total
            return 0

        lax.fori_loop(0, heads // group, step, 0)


def merge_call(heads, group, scale, q, pieces, states):
    tokens = q.shape[0]
    args = [q, *pieces, *[s[0] for s in states], *[s[1] for s in states]]
    vmem = pl.BlockSpec(memory_space=VMEM)
    pairs = tokens * sum(x.shape[0] for x in pieces) // 2 * heads * CHUNKS
    shapes = [pltpu.VMEM(s[0].shape, jnp.float32) for s in states]
    shapes.append(pltpu.VMEM((2 * CHUNKS * padded(heads), tokens), jnp.float32))
    return pl.pallas_call(
        lambda *refs: merge_kernel(heads, group, scale, len(pieces), *refs),
        in_specs=[vmem] * len(args),
        out_specs=[vmem] * len(shapes),
        out_shape=shapes,
        cost_estimate=pl.CostEstimate(
            flops=6 * pairs * HD, bytes_accessed=8 * tokens * heads * HD * 2, transcendentals=pairs
        ),
        compiler_params=pltpu.CompilerParams(vmem_limit_bytes=GRANT),
        name="merge",
    )(*[near_core(x) for x in args])


def final_kernel(heads, group, scale, n_sink, *refs):
    q, first, stat_o = refs[:3]
    accs, gots = refs[3 : 3 + CHUNKS], refs[3 + CHUNKS : 3 + 2 * CHUNKS]
    pieces = refs[3 + 2 * CHUNKS : 3 + 2 * CHUNKS + n_sink]
    rows = pieces[0].shape[0] // 2
    out, state, done, sems = refs[-4:]
    pad = padded(heads)
    wide = group * HD
    turns = heads // group

    def copy(turn):
        at = pl.ds(pl.multiple_of(turn * wide, HD), wide)
        return pltpu.make_async_copy(done.at[:, at], out.at[:, at], sems.at[turn])

    for c in range(CHUNKS):
        got = gots[c]
        part = [
            got[heads * HD + i * pad : heads * HD + (i + 1) * pad].astype(jnp.float32)
            for i in range(5)
        ]
        m1 = stat_o[2 * c * pad : (2 * c + 1) * pad]
        l1 = stat_o[(2 * c + 1) * pad : (2 * c + 2) * pad]
        m2 = jnp.where(first[0] > 0, part[0] + part[1] + part[2], NEG)
        l2 = part[3] + part[4]
        m12 = jnp.maximum(m1, m2)
        e1, e2 = jnp.exp2(m1 - m12), jnp.exp2(m2 - m12)
        for i, x in enumerate((m12, e1, e2, e1 * l1 + e2 * l2)):
            state[i * pad : (i + 1) * pad] = x

        def step(i, _):
            for g in range(group):
                head = i * group + g
                there, here = lanes(c * heads + head), lanes(head)
                m12, e1, e2, l12 = (state[pl.ds(n * pad + head, 1)] for n in range(4))
                k = jnp.concatenate([r[:rows, there] for r in pieces], axis=0)
                v = jnp.concatenate([r[rows:, there] for r in pieces], axis=0)
                s = dot(k, q[:, there], 1) * scale
                top = jnp.maximum(jnp.max(s, axis=0, keepdims=True), m12)
                p = jnp.exp2(s - top).astype(jnp.bfloat16)
                f = jnp.exp2(m12 - top)
                den = jnp.sum(p.astype(jnp.float32), axis=0, keepdims=True) + f * l12
                inv = 1.0 / den
                theirs = got[here].astype(jnp.float32)
                res = dot(v, p, 0) * inv + accs[c][here] * (f * e1 * inv) + theirs * (f * e2 * inv)
                done[:, there] = res.T.astype(done.dtype)
            copy(c * turns + i).start()
            return 0

        lax.fori_loop(0, turns, step, 0)

    def end(i, _):
        copy(i).wait()
        return 0

    lax.fori_loop(0, CHUNKS * turns, end, 0)


def final_call(heads, group, scale, q, accs, stat, gots, first, pieces):
    tokens, features = q.shape
    args = [q, first, stat, *accs, *gots, *pieces]
    vmem = pl.BlockSpec(memory_space=VMEM)
    specs = [vmem] * len(args)
    specs[1] = pl.BlockSpec(memory_space=pltpu.SMEM)
    args = [x if i == 1 else near_core(x) for i, x in enumerate(args)]
    pairs = tokens * sum(x.shape[0] for x in pieces) // 2 * heads * CHUNKS
    return pl.pallas_call(
        lambda *refs: final_kernel(heads, group, scale, len(pieces), *refs),
        in_specs=specs,
        out_specs=pl.BlockSpec(memory_space=pltpu.MemorySpace.HBM),
        out_shape=jax.ShapeDtypeStruct((tokens, features), q.dtype),
        scratch_shapes=[
            pltpu.VMEM((4 * padded(heads), tokens), jnp.float32),
            pltpu.VMEM((tokens, features), q.dtype),
            pltpu.SemaphoreType.DMA((CHUNKS * heads // group,)),
        ],
        cost_estimate=pl.CostEstimate(
            flops=6 * pairs * HD,
            bytes_accessed=16 * tokens * heads * HD * 2,
            transcendentals=pairs,
        ),
        compiler_params=pltpu.CompilerParams(vmem_limit_bytes=GRANT),
        name="final",
    )(*args)


def prepare_kernel(widths, rows, band_total, width_tiles, col_count, mask, info, q, k, v, *refs):
    near, later = refs[:CHUNKS], refs[CHUNKS : 2 * CHUNKS]
    cand, own, sems = refs[2 * CHUNKS :]
    tokens = q.shape[0]
    wide = widths[0]
    pairs = []
    at = pl.ds(pl.multiple_of(info[1] * rows, rows), rows)
    pairs += [(k.at[at], cand.at[:rows]), (v.at[at], cand.at[rows:])]
    for c in range(CHUNKS):
        part = slice(c * wide, (c + 1) * wide)
        pairs += [(k.at[:, part], near[c].at[:tokens]), (v.at[:, part], near[c].at[tokens:])]
    for c in range(CHUNKS):
        part = slice(c * wide, (c + 1) * wide)
        pairs.append((q.at[:, part], later[c].at[:, :wide]))
    copies = [pltpu.make_async_copy(x, y, sems.at[i]) for i, (x, y) in enumerate(pairs)]
    for copy in copies:
        copy.start()

    band = info[0]
    core = 1 - 2 * lax.rem(band, 2)
    lane = lax.broadcasted_iota(jnp.int32, (tokens, AUX), 1)
    token = lax.broadcasted_iota(jnp.int32, (tokens, AUX), 0)
    tile = lax.rem(token, col_count) // TC
    for slot in range(2):
        full = jnp.zeros((tokens, AUX), jnp.float32)
        for j, dh in enumerate((0, core, -core)):
            inside = (band + dh >= 0) & (band + dh < band_total)
            for cq in range(width_tiles):
                for ck in range(max(0, cq - 1), min(width_tiles, cq + 2)):
                    code = slot * 9 + (dh + 1) * 3 + ck - cq + 1
                    kept = mask[cq, code] > 0
                    if slot == 1 and j == 0 and ck == cq:
                        kept = True
                    value = jnp.where(inside & kept, 1.0, 0.0)
                    hit = (lane == j * width_tiles + ck) & (tile == cq)
                    full = jnp.where(hit, value, full)
        full = full.astype(jnp.bfloat16)
        if slot == 1:
            own[...] = full
        else:
            for c in range(CHUNKS):
                later[c][:, wide:] = full
    for copy in copies:
        copy.wait()


def prepare(q, k, v, mask, info, wide, rows, bands, col_count):
    tokens, features = q.shape
    hbm = pl.BlockSpec(memory_space=pltpu.MemorySpace.HBM)
    smem = pl.BlockSpec(memory_space=pltpu.SMEM)
    vmem = pl.BlockSpec(memory_space=VMEM)
    shapes = [pltpu.VMEM((2 * tokens, wide), q.dtype)] * CHUNKS
    shapes += [pltpu.VMEM((tokens, wide + AUX), q.dtype)] * CHUNKS
    shapes += [pltpu.VMEM((2 * rows, features), q.dtype), pltpu.VMEM((tokens, AUX), q.dtype)]
    args = [pltpu.with_memory_space_constraint(x, pltpu.MemorySpace.HBM) for x in (q, k, v)]
    return pl.pallas_call(
        lambda *refs: prepare_kernel((wide,), rows, bands, mask.shape[0], col_count, *refs),
        in_specs=[smem, smem, hbm, hbm, hbm],
        out_specs=[vmem] * len(shapes),
        out_shape=shapes,
        scratch_shapes=[pltpu.SemaphoreType.DMA((2 + 3 * CHUNKS,))],
        cost_estimate=pl.CostEstimate(
            flops=0, bytes_accessed=16 * tokens * features, transcendentals=0
        ),
        compiler_params=pltpu.CompilerParams(vmem_limit_bytes=GRANT),
        name="prepare",
    )(mask, info, *args)


def swap(x, axis, bit):
    count = lax.axis_size(axis)
    return lax.ppermute(x, axis, [(i, i ^ bit) for i in range(count)])


def shards(queries, keys, values, tile_mask, sink_frame):
    frames, row_count, col_count, features = queries.shape
    tokens = frames * row_count * col_count
    head_count = features // HD
    scale = math.log2(math.e) / math.sqrt(HD)
    times, bands = lax.axis_size("tm"), lax.axis_size("height")
    t, h = lax.axis_index("tm"), lax.axis_index("height")
    assert frames == TF and col_count == 2 * TC and tile_mask.shape[:2] == (1, 1) and head_count % CHUNKS == 0
    assert times & (times - 1) == 0 and bands & (bands - 1) == 0 and bands > 1
    heads = head_count // CHUNKS
    wide = heads * HD
    group = 5 if heads % 5 == 0 else 1

    q, k, v = (x.reshape(tokens, features) for x in (queries, keys, values))

    owner, local = sink_frame[0] // frames, sink_frame[0] % frames
    rows = row_count * col_count
    info = jnp.stack((h, local)).astype(jnp.int32)
    made = prepare(q, k, v, tile_mask[0, 0], info, wide, rows, bands, col_count)
    near_sent, q_sent = made[:CHUNKS], made[CHUNKS : 2 * CHUNKS]
    cand, flags_own = made[2 * CHUNKS :]

    odd = [(i, i + 1) for i in range(1, bands - 1, 2)]
    odd += [(j, i) for i, j in odd]
    sooner = [(i + 1, i) for i in range(times - 1)]
    near = [lax.ppermute(x, "height", odd) for x in near_sent]
    core_k, core_v = swap(k, "height", 1), swap(v, "height", 1)
    q_later = [lax.ppermute(x, "tm", sooner) for x in q_sent]

    bit = 1
    while bit < times:
        other = swap(cand, "tm", bit)
        have = (t ^ owner) // bit == 0
        cand = jnp.where(have, cand, other)
        bit *= 2
    pieces = [cand]
    bit = 2
    while bit < bands:
        pieces += [swap(x, "height", bit) for x in pieces]
        bit *= 2
    twins = [swap(x, "height", 1) for x in pieces]

    states, got = [], []
    for c in range(CHUNKS):
        bands_c = [(k, v, 0, 0, False), (core_k, core_v, 0, 0, False), (near[c], near[c], 0, 1, True)]
        (pay,) = attend(c, heads, group, scale, q_later[c], True, q_later[c], bands_c, False)
        got.append(lax.ppermute(pay, "tm", [(j, i) for i, j in sooner]))
        states.append(attend(c, heads, group, scale, q, False, flags_own, bands_c, True))
    first = (t > 0).astype(jnp.int32).reshape(1)
    early = max(1, len(pieces) - 1)
    *accs, stat = merge_call(heads, group, scale, q, pieces[:early] + twins[:early], states)
    out = final_call(heads, group, scale, q, accs, stat, got, first, pieces[early:] + twins[early:])
    return out.reshape(queries.shape)


def solution(mesh):
    spec = P("tm", "height", None, None)
    return jax.shard_map(
        shards,
        mesh=mesh,
        in_specs=(spec, spec, spec, spec, P()),
        out_specs=spec,
        check_vma=False,
    )
```

profile of v0, /device:TPU:1, one launch (start us, length us, event | category | flops | bytes accessed | tf_op | source)
XLA Modules:
  0.0 96.9 jit_solution(18440578462951874126)
XLA Ops:
  1.4 3.0 %prepare.1 = (bf16[256,1280]{1,0:T(8,128)(2,1)S(1)}, bf16[256,1280]{1,0:T(8,128)(2,1)S(1)}, bf16[128,1408]{1,0:T(8,128)(2,1)}, bf16[128,1408]{1,0:T(8,128)(2,1)S...) custom-call(s32[2,18]{1,0:T(2,128)S(1)} %bitcast.30, s32[2]{0:T(128)S(1)} %pad_add_fusion.refs_1_, ...), custom_call_target="tpu_custom_call" | custom-call | bytes 5242880 | tf_op jit(solution)/shard_map/prepare/pallas_call | solution.py:314
  4.5 0.8 copy-done.12
  6.9 2.1 %collective-permute-start = (bf16[64,2560]{1,0:T(8,128)(2,1)S(1)}, bf16[64,2560]{1,0:T(8,128)(2,1)S(1)}, u32[]{:S(2)}, u32[]{:S(2)}) collective-permute-start(bf16[64,2560]{1,0:T(8,128)(2,1)S(1)} %get-tuple-element.18), channel_id=1, source_target_pairs={{0,8},{8,0},{16,24},{24,16},{1,9},{9,1},{17,25},{25,17},{2,10},{10... | collective-permute-start | bytes 983048 | tf_op jit(solution)/shard_map/ppermute | solution.py:330
  9.0 7.4 %collective-permute-done = bf16[64,2560]{1,0:T(8,128)(2,1)S(1)} collective-permute-done((bf16[64,2560]{1,0:T(8,128)(2,1)S(1)}, bf16[64,2560]{1,0:T(8,128)(2,1)S(1)}, u32[]{:S(2)}, u32[]{:S(2)}) %collective-permute-start) | collective-permute-done | bytes 327712 | tf_op jit(solution)/shard_map/ppermute | solution.py:330
  17.2 2.2 %collective-permute-start.1 = (bf16[64,2560]{1,0:T(8,128)(2,1)}, bf16[64,2560]{1,0:T(8,128)(2,1)}, u32[]{:S(2)}, u32[]{:S(2)}) collective-permute-start(bf16[64,2560]{1,0:T(8,128)(2,1)} %broadcast_select_fusion), channel_id=1, source_target_pairs={{0,16},{8,24},{16,0},{24,8},{1,17},{9,25},{17,1},{25,9},{2,18},{10... | collective-permute-start | bytes 983048 | tf_op jit(solution)/shard_map/ppermute | solution.py:330
  19.4 1.8 %collective-permute-start.7 = (bf16[128,2560]{1,0:T(8,128)(2,1)S(1)}, bf16[128,2560]{1,0:T(8,128)(2,1)S(1)}, u32[]{:S(2)}, u32[]{:S(2)}) collective-permute-start(bf16[128,2560]{1,0:T(8,128)(2,1)S(1)} %bitcast.19), channel_id=1, source_target_pairs={{0,1},{1,0},{2,3},{3,2},{4,5},{5,4},{6,7},{7,6},{8,9},{9,8},{10,11... | collective-permute-start | bytes 1966088 | tf_op jit(solution)/shard_map/ppermute | solution.py:330
  21.3 1.3 %collective-permute-start.11 = (bf16[128,1408]{1,0:T(8,128)(2,1)}, bf16[128,1408]{1,0:T(8,128)(2,1)}, u32[]{:S(2)}, u32[]{:S(2)}) collective-permute-start(bf16[128,1408]{1,0:T(8,128)(2,1)} %get-tuple-element.29), channel_id=1, source_target_pairs={{8,0},{16,8},{24,16},{9,1},{17,9},{25,17},{10,2},{18,10},{26,18},{... | collective-permute-start | bytes 1081352 | tf_op jit(solution)/shard_map/ppermute | solution.py:360
  22.5 3.4 %collective-permute-start.8 = (bf16[256,1280]{1,0:T(8,128)(2,1)}, bf16[256,1280]{1,0:T(8,128)(2,1)S(1)}, u32[]{:S(2)}, u32[]{:S(2)}) collective-permute-start(bf16[256,1280]{1,0:T(8,128)(2,1)} %copy-done.13), channel_id=1, source_target_pairs={{1,2},{3,4},{5,6},{2,1},{4,3},{6,5},{9,10},{11,12},{13,14},{10,9},... | collective-permute-start | bytes 1966088 | tf_op jit(solution)/shard_map/ppermute | solution.py:358
  26.0 8.2 %collective-permute-done.1 = bf16[64,2560]{1,0:T(8,128)(2,1)} collective-permute-done((bf16[64,2560]{1,0:T(8,128)(2,1)}, bf16[64,2560]{1,0:T(8,128)(2,1)}, u32[]{:S(2)}, u32[]{:S(2)}) %collective-permute-start.1) | collective-permute-done | bytes 327712 | tf_op jit(solution)/shard_map/ppermute | solution.py:330
  34.2 5.5 %collective-permute-start.10 = (bf16[256,1280]{1,0:T(8,128)(2,1)}, bf16[256,1280]{1,0:T(8,128)(2,1)S(1)}, u32[]{:S(2)}, u32[]{:S(2)}) collective-permute-start(bf16[256,1280]{1,0:T(8,128)(2,1)} %copy-done.12), channel_id=1, source_target_pairs={{1,2},{3,4},{5,6},{2,1},{4,3},{6,5},{9,10},{11,12},{13,14},{10,9},... | collective-permute-start | bytes 1966088 | tf_op jit(solution)/shard_map/ppermute | solution.py:358
  39.7 1.0 %broadcast_select_fusion.1.refs_1_ = bf16[64,2560]{1,0:T(8,128)(2,1)S(1)} fusion(bf16[64,2560]{1,0:T(8,128)(2,1)} %broadcast_select_fusion, bf16[64,2560]{1,0:T(8,128)(2,1)} %collective-permute-done.1, pred[]{:T(512)S(6)} %eq.8), kind=kLoop, calls=%fused_computation.1 | loop fusion | flops 163840 | bytes 983041 | tf_op jit(solution)/shard_map/jit(_where)/select_n | solution.py:366
  40.8 1.3 %collective-permute-start.2 = (bf16[64,2560]{1,0:T(8,128)(2,1)S(1)}, bf16[64,2560]{1,0:T(8,128)(2,1)}, u32[]{:S(2)}, u32[]{:S(2)}) collective-permute-start(bf16[64,2560]{1,0:T(8,128)(2,1)S(1)} %broadcast_select_fusion.1.refs_1_), channel_id=1, source_target_pairs={{0,2},{1,3},{2,0},{3,1},{4,6},{5,7},{6,4},{7,5},{8,10},{9,11},{10,... | collective-permute-start | bytes 983048 | tf_op jit(solution)/shard_map/ppermute | solution.py:330
  42.0 1.3 %collective-permute-start.13 = (bf16[128,1408]{1,0:T(8,128)(2,1)S(1)}, bf16[128,1408]{1,0:T(8,128)(2,1)S(1)}, u32[]{:S(2)}, u32[]{:S(2)}) collective-permute-start(bf16[128,1408]{1,0:T(8,128)(2,1)S(1)} %copy-done.15), channel_id=1, source_target_pairs={{8,0},{16,8},{24,16},{9,1},{17,9},{25,17},{10,2},{18,10},{26,18},{... | collective-permute-start | bytes 1081352 | tf_op jit(solution)/shard_map/ppermute | solution.py:360
  43.5 1.1 %collective-permute-start.4 = (bf16[64,2560]{1,0:T(8,128)(2,1)S(1)}, bf16[64,2560]{1,0:T(8,128)(2,1)S(1)}, u32[]{:S(2)}, u32[]{:S(2)}) collective-permute-start(bf16[64,2560]{1,0:T(8,128)(2,1)S(1)} %broadcast_select_fusion.1.refs_1_), channel_id=1, source_target_pairs={{0,1},{1,0},{2,3},{3,2},{4,5},{5,4},{6,7},{7,6},{8,9},{9,8},{10,11... | collective-permute-start | bytes 983048 | tf_op jit(solution)/shard_map/ppermute | solution.py:330
  44.6 18.3 %collective-permute-done.2.refs_2_ = bf16[64,2560]{1,0:T(8,128)(2,1)} collective-permute-done((bf16[64,2560]{1,0:T(8,128)(2,1)S(1)}, bf16[64,2560]{1,0:T(8,128)(2,1)}, u32[]{:S(2)}, u32[]{:S(2)}) %collective-permute-start.2) | collective-permute-done | bytes 327712 | tf_op jit(solution)/shard_map/ppermute | solution.py:330
  62.9 3.2 %attend.6 = bf16[1360,128]{1,0:T(8,128)(2,1)} custom-call(bf16[128,1408]{1,0:T(8,128)(2,1)} %collective-permute-done.11.refs_0_.refs_1_, bf16[128,1408]{1,0:T(8,128)(2,1)} %collective-permute-done.11.refs_0_.refs_1_, bf16[128,2560]{1,0:T(8,128)(2,1)S(1)} %bitcast.20, bf16[128,2560]{1,0:T(8,128)(2,1)S(1)} %collective-permute-done.7.refs_3_, ...), custom_call_target="tpu_custom_call" | custom-call | flops 377487360 | bytes 3276800 | tf_op jit(solution)/shard_map/attend/pallas_call | solution.py:111
  66.9 5.3 %collective-permute-start.12 = (bf16[1360,128]{1,0:T(8,128)(2,1)}, bf16[1360,128]{1,0:T(8,128)(2,1)}, u32[]{:S(2)}, u32[]{:S(2)}) collective-permute-start(bf16[1360,128]{1,0:T(8,128)(2,1)} %attend.6), channel_id=1, source_target_pairs={{0,8},{8,16},{16,24},{1,9},{9,17},{17,25},{2,10},{10,18},{18,26},{... | collective-permute-start | bytes 1044488 | tf_op jit(solution)/shard_map/ppermute | solution.py:379
  73.1 2.1 %attend.7 = bf16[1360,128]{1,0:T(8,128)(2,1)} custom-call(bf16[128,1408]{1,0:T(8,128)(2,1)S(1)} %collective-permute-done.13.refs_0_.refs_1_, bf16[128,1408]{1,0:T(8,128)(2,1)S(1)} %collective-permute-done.13.refs_0_.refs_1_, bf16[128,2560]{1,0:T(8,128)(2,1)S(1)} %bitcast.21, bf16[128,2560]{1,0:T(8,128)(2,1)S(1)} %collective-permute-done.7.refs_3_, ...), custom_call_target="tpu_custom_call" | custom-call | flops 377487360 | bytes 3276800 | tf_op jit(solution)/shard_map/attend/pallas_call | solution.py:111
  76.0 3.3 %collective-permute-start.14 = (bf16[1360,128]{1,0:T(8,128)(2,1)}, bf16[1360,128]{1,0:T(8,128)(2,1)}, u32[]{:S(2)}, u32[]{:S(2)}) collective-permute-start(bf16[1360,128]{1,0:T(8,128)(2,1)} %attend.7), channel_id=1, source_target_pairs={{0,8},{8,16},{16,24},{1,9},{9,17},{17,25},{2,10},{10,18},{18,26},{... | collective-permute-start | bytes 1044488 | tf_op jit(solution)/shard_map/ppermute | solution.py:379
  80.0 1.1 %copy-done.4 = bf16[256,1280]{1,0:T(8,128)(2,1)S(1)} copy-done((bf16[256,1280]{1,0:T(8,128)(2,1)S(1)}, bf16[256,1280]{1,0:T(8,128)(2,1)}, u32[]{:S(2)}) %copy-start.4) | copy-done | bytes 655384
  81.1 1.4 %attend.4 = (f32[1280,128]{1,0:T(8,128)S(1)}, f32[32,128]{1,0:T(8,128)S(1)}) custom-call(bf16[128,2560]{1,0:T(8,128)(2,1)S(1)} %bitcast.14, bf16[128,128]{1,0:T(8,128)(2,1)S(1)} %get-tuple-element.19.refs_1_, bf16[128,2560]{1,0:T(8,128)(2,1)S(1)} %bitcast.22, bf16[128,2560]{1,0:T(8,128)(2,1)S(1)} %collective-permute-done.7.refs_3_, ...), custom_call_target="tpu_custom_call" | custom-call | flops 377487360 | bytes 3276800 | tf_op jit(solution)/shard_map/attend/pallas_call | solution.py:111
  82.5 1.4 %attend.5 = (f32[1280,128]{1,0:T(8,128)S(1)}, f32[32,128]{1,0:T(8,128)S(1)}) custom-call(bf16[128,2560]{1,0:T(8,128)(2,1)S(1)} %bitcast.15, bf16[128,128]{1,0:T(8,128)(2,1)S(1)} %get-tuple-element.19.refs_1_, bf16[128,2560]{1,0:T(8,128)(2,1)S(1)} %bitcast.23, bf16[128,2560]{1,0:T(8,128)(2,1)S(1)} %collective-permute-done.7.refs_3_, ...), custom_call_target="tpu_custom_call" | custom-call | flops 377487360 | bytes 3276800 | tf_op jit(solution)/shard_map/attend/pallas_call | solution.py:111
  84.0 6.3 %merge.1 = (f32[1280,128]{1,0:T(8,128)S(1)}, f32[1280,128]{1,0:T(8,128)S(1)}, f32[64,128]{1,0:T(8,128)S(1)}) custom-call(bf16[128,2560]{1,0:T(8,128)(2,1)S(1)} %bitcast.16, bf16[64,2560]{1,0:T(8,128)(2,1)S(1)} %copy-done.8, bf16[64,2560]{1,0:T(8,128)(2,1)} %collective-permute-done.2.refs_2_, bf16[64,2560]{1,0:T(8,128)(2,1)} %collective-permute-done.3.refs_3_, ...), custom_call_target="tpu_custom_call" | custom-call | flops 377487360 | bytes 2621440 | tf_op jit(solution)/shard_map/merge/pallas_call | solution.py:161
  90.3 6.6 %final.1 = bf16[128,2560]{1,0:T(8,128)(2,1)} custom-call(bf16[128,2560]{1,0:T(8,128)(2,1)S(1)} %bitcast.17, s32[1]{0:T(128)} %bitcast.1.refs_1_, f32[64,128]{1,0:T(8,128)S(1)} %get-tuple-element.26.refs_2_, f32[1280,128]{1,0:T(8,128)S(1)} %get-tuple-element.27.refs_3_, f32[1280,128]{1,0:T(8,128)S(1)} %get-tuple-element.28.refs_4_, ...), custom_call_target="tpu_custom_call" | custom-call | flops 125829120 | bytes 5242880 | tf_op jit(solution)/shard_map/final/pallas_call | solution.py:239
  (52 shorter events, 6.5 us)
Async XLA Ops:
  1.4 19.8 %copy-start.2 = (bf16[4,2,16,2560]{3,2,1,0:T(8,128)(2,1)S(1)}, bf16[4,2,16,2560]{3,2,1,0:T(8,128)(2,1)}, u32[]{:S(2)}) copy-start(bf16[4,2,16,2560]{3,2,1,0:T(8,128)(2,1)} %param.7) | copy-start | bytes 1966084
  6.9 12.5 %copy-start.1 = (bf16[4,2,16,2560]{3,2,1,0:T(8,128)(2,1)S(1)}, bf16[4,2,16,2560]{3,2,1,0:T(8,128)(2,1)}, u32[]{:S(2)}) copy-start(bf16[4,2,16,2560]{3,2,1,0:T(8,128)(2,1)} %param.6) | copy-start | bytes 1966084
  6.9 9.5 %collective-permute-start = (bf16[64,2560]{1,0:T(8,128)(2,1)S(1)}, bf16[64,2560]{1,0:T(8,128)(2,1)S(1)}, u32[]{:S(2)}, u32[]{:S(2)}) collective-permute-start(bf16[64,2560]{1,0:T(8,128)(2,1)S(1)} %get-tuple-element.18), channel_id=1, source_target_pairs={{0,8},{8,0},{16,24},{24,16},{1,9},{9,1},{17,25},{25,17},{2,10},{10... | collective-permute-start | bytes 983048 | tf_op jit(solution)/shard_map/ppermute | solution.py:330
  17.2 17.0 %collective-permute-start.1 = (bf16[64,2560]{1,0:T(8,128)(2,1)}, bf16[64,2560]{1,0:T(8,128)(2,1)}, u32[]{:S(2)}, u32[]{:S(2)}) collective-permute-start(bf16[64,2560]{1,0:T(8,128)(2,1)} %broadcast_select_fusion), channel_id=1, source_target_pairs={{0,16},{8,24},{16,0},{24,8},{1,17},{9,25},{17,1},{25,9},{2,18},{10... | collective-permute-start | bytes 983048 | tf_op jit(solution)/shard_map/ppermute | solution.py:330
  19.4 22.7 %collective-permute-start.7 = (bf16[128,2560]{1,0:T(8,128)(2,1)S(1)}, bf16[128,2560]{1,0:T(8,128)(2,1)S(1)}, u32[]{:S(2)}, u32[]{:S(2)}) collective-permute-start(bf16[128,2560]{1,0:T(8,128)(2,1)S(1)} %bitcast.19), channel_id=1, source_target_pairs={{0,1},{1,0},{2,3},{3,2},{4,5},{5,4},{6,7},{7,6},{8,9},{9,8},{10,11... | collective-permute-start | bytes 1966088 | tf_op jit(solution)/shard_map/ppermute | solution.py:330
  21.2 22.1 %collective-permute-start.9 = (bf16[128,2560]{1,0:T(8,128)(2,1)S(1)}, bf16[128,2560]{1,0:T(8,128)(2,1)S(1)}, u32[]{:S(2)}, u32[]{:S(2)}) collective-permute-start(bf16[128,2560]{1,0:T(8,128)(2,1)S(1)} %bitcast.25), channel_id=1, source_target_pairs={{0,1},{1,0},{2,3},{3,2},{4,5},{5,4},{6,7},{7,6},{8,9},{9,8},{10,11... | collective-permute-start | bytes 1966088 | tf_op jit(solution)/shard_map/ppermute | solution.py:330
  21.3 19.5 %collective-permute-start.11 = (bf16[128,1408]{1,0:T(8,128)(2,1)}, bf16[128,1408]{1,0:T(8,128)(2,1)}, u32[]{:S(2)}, u32[]{:S(2)}) collective-permute-start(bf16[128,1408]{1,0:T(8,128)(2,1)} %get-tuple-element.29), channel_id=1, source_target_pairs={{8,0},{16,8},{24,16},{9,1},{17,9},{25,17},{10,2},{18,10},{26,18},{... | collective-permute-start | bytes 1081352 | tf_op jit(solution)/shard_map/ppermute | solution.py:360
  22.5 20.9 %collective-permute-start.8 = (bf16[256,1280]{1,0:T(8,128)(2,1)}, bf16[256,1280]{1,0:T(8,128)(2,1)S(1)}, u32[]{:S(2)}, u32[]{:S(2)}) collective-permute-start(bf16[256,1280]{1,0:T(8,128)(2,1)} %copy-done.13), channel_id=1, source_target_pairs={{1,2},{3,4},{5,6},{2,1},{4,3},{6,5},{9,10},{11,12},{13,14},{10,9},... | collective-permute-start | bytes 1966088 | tf_op jit(solution)/shard_map/ppermute | solution.py:358
  34.2 7.9 %copy-start.15 = (bf16[128,1408]{1,0:T(8,128)(2,1)S(1)}, bf16[128,1408]{1,0:T(8,128)(2,1)}, u32[]{:S(2)}) copy-start(bf16[128,1408]{1,0:T(8,128)(2,1)} %copy-done.14) | copy-start | bytes 1081348
  34.2 38.1 %collective-permute-start.10 = (bf16[256,1280]{1,0:T(8,128)(2,1)}, bf16[256,1280]{1,0:T(8,128)(2,1)S(1)}, u32[]{:S(2)}, u32[]{:S(2)}) collective-permute-start(bf16[256,1280]{1,0:T(8,128)(2,1)} %copy-done.12), channel_id=1, source_target_pairs={{1,2},{3,4},{5,6},{2,1},{4,3},{6,5},{9,10},{11,12},{13,14},{10,9},... | collective-permute-start | bytes 1966088 | tf_op jit(solution)/shard_map/ppermute | solution.py:358
  40.7 25.4 %copy-start.7 = (bf16[64,2560]{1,0:T(8,128)(2,1)}, bf16[64,2560]{1,0:T(8,128)(2,1)S(1)}, u32[]{:S(2)}) copy-start(bf16[64,2560]{1,0:T(8,128)(2,1)S(1)} %broadcast_select_fusion.1.refs_1_) | copy-start | bytes 983044
  40.8 22.1 %collective-permute-start.2 = (bf16[64,2560]{1,0:T(8,128)(2,1)S(1)}, bf16[64,2560]{1,0:T(8,128)(2,1)}, u32[]{:S(2)}, u32[]{:S(2)}) collective-permute-start(bf16[64,2560]{1,0:T(8,128)(2,1)S(1)} %broadcast_select_fusion.1.refs_1_), channel_id=1, source_target_pairs={{0,2},{1,3},{2,0},{3,1},{4,6},{5,7},{6,4},{7,5},{8,10},{9,11},{10,... | collective-permute-start | bytes 983048 | tf_op jit(solution)/shard_map/ppermute | solution.py:330
  42.0 24.9 %collective-permute-start.13 = (bf16[128,1408]{1,0:T(8,128)(2,1)S(1)}, bf16[128,1408]{1,0:T(8,128)(2,1)S(1)}, u32[]{:S(2)}, u32[]{:S(2)}) collective-permute-start(bf16[128,1408]{1,0:T(8,128)(2,1)S(1)} %copy-done.15), channel_id=1, source_target_pairs={{8,0},{16,8},{24,16},{9,1},{17,9},{25,17},{10,2},{18,10},{26,18},{... | collective-permute-start | bytes 1081352 | tf_op jit(solution)/shard_map/ppermute | solution.py:360
  43.3 29.7 %collective-permute-start.3 = (bf16[64,2560]{1,0:T(8,128)(2,1)S(1)}, bf16[64,2560]{1,0:T(8,128)(2,1)}, u32[]{:S(2)}, u32[]{:S(2)}) collective-permute-start(bf16[64,2560]{1,0:T(8,128)(2,1)S(1)} %broadcast_select_fusion.1.refs_1_), channel_id=1, source_target_pairs={{0,4},{1,5},{2,6},{3,7},{4,0},{5,1},{6,2},{7,3},{8,12},{9,13},{10,... | collective-permute-start | bytes 983048 | tf_op jit(solution)/shard_map/ppermute | solution.py:330
  43.5 31.8 %collective-permute-start.4 = (bf16[64,2560]{1,0:T(8,128)(2,1)S(1)}, bf16[64,2560]{1,0:T(8,128)(2,1)S(1)}, u32[]{:S(2)}, u32[]{:S(2)}) collective-permute-start(bf16[64,2560]{1,0:T(8,128)(2,1)S(1)} %broadcast_select_fusion.1.refs_1_), channel_id=1, source_target_pairs={{0,1},{1,0},{2,3},{3,2},{4,5},{5,4},{6,7},{7,6},{8,9},{9,8},{10,11... | collective-permute-start | bytes 983048 | tf_op jit(solution)/shard_map/ppermute | solution.py:330
  62.9 16.5 %collective-permute-start.15 = (bf16[64,2560]{1,0:T(8,128)(2,1)}, bf16[64,2560]{1,0:T(8,128)(2,1)}, u32[]{:S(2)}, u32[]{:S(2)}) collective-permute-start(bf16[64,2560]{1,0:T(8,128)(2,1)} %collective-permute-done.2.refs_2_), channel_id=1, source_target_pairs={{0,4},{1,5},{2,6},{3,7},{4,0},{5,1},{6,2},{7,3},{8,12},{9,13},{10,... | collective-permute-start | bytes 983048 | tf_op jit(solution)/shard_map/ppermute | solution.py:330
  66.9 13.1 %copy-start = (bf16[4,2,16,2560]{3,2,1,0:T(8,128)(2,1)S(1)}, bf16[4,2,16,2560]{3,2,1,0:T(8,128)(2,1)}, u32[]{:S(2)}) copy-start(bf16[4,2,16,2560]{3,2,1,0:T(8,128)(2,1)} %param.5) | copy-start | bytes 1966084
  66.9 23.3 %collective-permute-start.12 = (bf16[1360,128]{1,0:T(8,128)(2,1)}, bf16[1360,128]{1,0:T(8,128)(2,1)}, u32[]{:S(2)}, u32[]{:S(2)}) collective-permute-start(bf16[1360,128]{1,0:T(8,128)(2,1)} %attend.6), channel_id=1, source_target_pairs={{0,8},{8,16},{16,24},{1,9},{9,17},{17,25},{2,10},{10,18},{18,26},{... | collective-permute-start | bytes 1044488 | tf_op jit(solution)/shard_map/ppermute | solution.py:379
  72.3 3.0 %copy-start.5 = (bf16[256,1280]{1,0:T(8,128)(2,1)}, bf16[256,1280]{1,0:T(8,128)(2,1)S(1)}, u32[]{:S(2)}) copy-start(bf16[256,1280]{1,0:T(8,128)(2,1)S(1)} %collective-permute-done.10.refs_4_.refs_7_) | copy-start | bytes 1966084
  72.3 11.7 %collective-permute-start.5 = (bf16[64,2560]{1,0:T(8,128)(2,1)}, bf16[64,2560]{1,0:T(8,128)(2,1)}, u32[]{:S(2)}, u32[]{:S(2)}) collective-permute-start(bf16[64,2560]{1,0:T(8,128)(2,1)} %collective-permute-done.2.refs_2_), channel_id=1, source_target_pairs={{0,1},{1,0},{2,3},{3,2},{4,5},{5,4},{6,7},{7,6},{8,9},{9,8},{10,11... | collective-permute-start | bytes 983048 | tf_op jit(solution)/shard_map/ppermute | solution.py:330
  73.1 10.9 %collective-permute-start.6 = (bf16[64,2560]{1,0:T(8,128)(2,1)}, bf16[64,2560]{1,0:T(8,128)(2,1)}, u32[]{:S(2)}, u32[]{:S(2)}) collective-permute-start(bf16[64,2560]{1,0:T(8,128)(2,1)} %collective-permute-done.3.refs_3_), channel_id=1, source_target_pairs={{0,1},{1,0},{2,3},{3,2},{4,5},{5,4},{6,7},{7,6},{8,9},{9,8},{10,11... | collective-permute-start | bytes 983048 | tf_op jit(solution)/shard_map/ppermute | solution.py:330
  76.0 14.2 %collective-permute-start.14 = (bf16[1360,128]{1,0:T(8,128)(2,1)}, bf16[1360,128]{1,0:T(8,128)(2,1)}, u32[]{:S(2)}, u32[]{:S(2)}) collective-permute-start(bf16[1360,128]{1,0:T(8,128)(2,1)} %attend.7), channel_id=1, source_target_pairs={{0,8},{8,16},{16,24},{1,9},{9,17},{17,25},{2,10},{10,18},{18,26},{... | collective-permute-start | bytes 1044488 | tf_op jit(solution)/shard_map/ppermute | solution.py:379
  79.3 11.0 %collective-permute-start.16 = (bf16[64,2560]{1,0:T(8,128)(2,1)}, bf16[64,2560]{1,0:T(8,128)(2,1)}, u32[]{:S(2)}, u32[]{:S(2)}) collective-permute-start(bf16[64,2560]{1,0:T(8,128)(2,1)} %collective-permute-done.15.refs_7_), channel_id=1, source_target_pairs={{0,1},{1,0},{2,3},{3,2},{4,5},{5,4},{6,7},{7,6},{8,9},{9,8},{10,11... | collective-permute-start | bytes 983048 | tf_op jit(solution)/shard_map/ppermute | solution.py:330
  82.5 1.5 %copy-start.8 = (bf16[64,2560]{1,0:T(8,128)(2,1)S(1)}, bf16[64,2560]{1,0:T(8,128)(2,1)}, u32[]{:S(2)}) copy-start(bf16[64,2560]{1,0:T(8,128)(2,1)} %copy-done.7) | copy-start | bytes 983044
  (9 other events, 8.6 us)
where the time goes:
time: 97.7 us; the launch traced here: 96.9 us
  waiting for transfers between devices  33.9 us (35%)
  starting transfers between devices  30.4 us (31%)
  Pallas kernels  24.1 us (25%)
  local copies, waits for them, and re-layouts  5.81 us (6%)
  other arithmetic  1.86 us (2%)
    ppermute x11, waiting for transfers between devices, swap(): return lax.ppermute(x, axis, [(i, i ^ bit) for i in range(count)])  33.9 us
    ppermute x11, starting transfers between devices, swap(): return lax.ppermute(x, axis, [(i, i ^ bit) for i in range(count)])  10.3 us
    ppermute x2, starting transfers between devices, shards(): near = [lax.ppermute(x, 'height', odd) for x in near_sent]  8.96 us
    ppermute x2, starting transfers between devices, shards(): got.append(lax.ppermute(pay, 'tm', [(j, i) for i, j in sooner]))  8.6 us
    pallas_call x4, Pallas kernels, attend(): pl.pallas_call(lambda *refs: attend_kernel(chunk, heads, group, scale, pl...  8.19 us
    pallas_call x1, Pallas kernels, final_call(): pl.pallas_call(lambda *refs: final_kernel(heads, group, scale, len(pieces...  6.63 us
    pallas_call x1, Pallas kernels, merge_call(): pl.pallas_call(lambda *refs: merge_kernel(heads, group, scale, len(pieces...  6.26 us
    unnamed x32, local copies, waits for them, and re-layouts  5.81 us
  transfers between devices with their start and end apart: 17, of which 3 were waited for; matrix products, arithmetic and copies ran while one was open for 1% of the time, Pallas kernels for 15%

commit v1 on v0

v1 whole, which is shorter than its diff:
```python
import math

import jax
import jax.numpy as jnp
from jax import lax
from jax.experimental import pallas as pl
from jax.experimental.pallas import tpu as pltpu
from jax.sharding import PartitionSpec as P


HD = 128
TF = 4
TC = 8
CHUNKS = 2
NEG = -1e30
AUX = 128
GRANT = 12 << 20


def split3(x):
    hi = x.astype(jnp.bfloat16).astype(jnp.float32)
    mid = (x - hi).astype(jnp.bfloat16).astype(jnp.float32)
    return hi, mid, x - hi - mid


def dot(x, y, contract):
    dims = (((contract,), (contract,)), ((), ()))
    return lax.dot_general(x, y, dims, preferred_element_type=jnp.float32)


VMEM = pltpu.MemorySpace.VMEM


def near_core(x):
    return pltpu.with_memory_space_constraint(x, VMEM)


def lanes(head):
    return pl.ds(pl.multiple_of(head * HD, HD), HD)


def attend_kernel(chunk, heads, group, scale, places, n_arrays, own, *refs):
    arrays = refs[:n_arrays]
    q, q_part = arrays[0], not own
    flags = arrays[1] if own else q
    acc, stat, bias = refs[n_arrays:]
    tokens = q.shape[0]
    pad = stat.shape[0] // 2

    second = (lax.broadcasted_iota(jnp.int32, (tokens, tokens), 0) // TC) % 2 == 1
    kept = jnp.where(flags[:, flags.shape[1] - AUX :].astype(jnp.float32).T > 0.5, 0.0, NEG)
    for j in range(len(places)):
        one = jnp.broadcast_to(kept[2 * j : 2 * j + 1], second.shape)
        two = jnp.broadcast_to(kept[2 * j + 1 : 2 * j + 2], second.shape)
        bias[j * tokens : (j + 1) * tokens] = jnp.where(second, two, one)
    stat[...] = jnp.zeros_like(stat)

    def step(i, _):
        for g in range(group):
            head = i * group + g
            there = lanes(chunk * heads + head)
            here = lanes(head)

            def block(n, row, part):
                return arrays[n][row * tokens : (row + 1) * tokens, here if part else there]

            k = jnp.concatenate([block(nk, rk, part) for nk, rk, _, _, part in places], axis=0)
            v = jnp.concatenate([block(nv, rv, part) for _, _, nv, rv, part in places], axis=0)
            s = dot(k, q[:, here if q_part else there], 1) * scale + bias[...]
            m = jnp.max(s, axis=0, keepdims=True)
            p = jnp.exp2(s - m).astype(jnp.bfloat16)
            acc[here] = dot(v, p, 0).astype(acc.dtype)
            stat[pl.ds(head, 1)] = m
            stat[pl.ds(pad + head, 1)] = jnp.sum(p.astype(jnp.float32), axis=0, keepdims=True)
        return 0

    lax.fori_loop(0, heads // group, step, 0)
    if not own:
        parts = split3(stat[:pad]) + split3(stat[pad:])[:2]
        for i, part in enumerate(parts):
            acc[heads * HD + i * pad : heads * HD + (i + 1) * pad] = part.astype(acc.dtype)


def padded(heads):
    return -(-heads // 16) * 16


def attend(chunk, heads, group, scale, q, flags, bands):
    tokens, pad = q.shape[0], padded(heads)
    own = flags is not None
    args = [q, flags] if own else [q]
    places = []
    for k, rk, v, rv, part in bands:
        where = []
        for x in (k, v):
            if not any(x is y for y in args):
                args.append(x)
            where.append([x is y for y in args].index(True))
        places.append((where[0], rk, where[1], rv, part))
    keys = len(bands) * tokens
    stat = (2 * pad, tokens)
    vmem = pl.BlockSpec(memory_space=VMEM)
    if own:
        out_shape = (pltpu.VMEM((heads * HD, tokens), jnp.float32), pltpu.VMEM(stat, jnp.float32))
        scratch = []
    else:
        out_shape = (pltpu.VMEM((heads * HD + 5 * pad, tokens), jnp.bfloat16),)
        scratch = [pltpu.VMEM(stat, jnp.float32)]
    pairs = tokens * keys * heads
    return pl.pallas_call(
        lambda *refs: attend_kernel(chunk, heads, group, scale, places, len(args), own, *refs),
        in_specs=[vmem] * len(args),
        out_specs=(vmem,) * len(out_shape),
        out_shape=out_shape,
        scratch_shapes=scratch + [pltpu.VMEM((keys, tokens), jnp.float32)],
        cost_estimate=pl.CostEstimate(
            flops=6 * pairs * HD, bytes_accessed=10 * tokens * heads * HD * 2, transcendentals=pairs
        ),
        compiler_params=pltpu.CompilerParams(vmem_limit_bytes=GRANT),
        name="attend",
    )(*[near_core(x) for x in args])


def final_kernel(heads, group, scale, n_sink, *refs):
    q = refs[0]
    accs, stats, gots = (refs[1 + i * CHUNKS :][:CHUNKS] for i in range(3))
    pieces = refs[1 + 3 * CHUNKS : 1 + 3 * CHUNKS + n_sink]
    rows = pieces[0].shape[0] // 2
    out, state, done, sems = refs[-4:]
    pad = padded(heads)
    wide = group * HD
    turns = heads // group

    def copy(turn):
        at = pl.ds(pl.multiple_of(turn * wide, HD), wide)
        return pltpu.make_async_copy(done.at[:, at], out.at[:, at], sems.at[turn])

    for c in range(CHUNKS):
        got = gots[c]
        part = [
            got[heads * HD + i * pad : heads * HD + (i + 1) * pad].astype(jnp.float32)
            for i in range(5)
        ]
        m1, l1 = stats[c][:pad], stats[c][pad:]
        l2 = part[3] + part[4]
        m2 = jnp.where(l2 > 0, part[0] + part[1] + part[2], NEG)
        m12 = jnp.maximum(m1, m2)
        e1, e2 = jnp.exp2(m1 - m12), jnp.exp2(m2 - m12)
        for i, x in enumerate((m12, e1, e2, e1 * l1 + e2 * l2)):
            state[i * pad : (i + 1) * pad] = x

        def step(i, _):
            for g in range(group):
                head = i * group + g
                there, here = lanes(c * heads + head), lanes(head)
                m12, e1, e2, l12 = (state[pl.ds(n * pad + head, 1)] for n in range(4))
                k = jnp.concatenate([r[:rows, there] for r in pieces], axis=0)
                v = jnp.concatenate([r[rows:, there] for r in pieces], axis=0)
                s = dot(k, q[:, there], 1) * scale
                top = jnp.maximum(jnp.max(s, axis=0, keepdims=True), m12)
                p = jnp.exp2(s - top).astype(jnp.bfloat16)
                f = jnp.exp2(m12 - top)
                den = jnp.sum(p.astype(jnp.float32), axis=0, keepdims=True) + f * l12
                inv = 1.0 / den
                theirs = got[here].astype(jnp.float32)
                res = dot(v, p, 0) * inv + accs[c][here] * (f * e1 * inv) + theirs * (f * e2 * inv)
                done[:, there] = res.T.astype(done.dtype)
            copy(c * turns + i).start()
            return 0

        lax.fori_loop(0, turns, step, 0)

    def end(i, _):
        copy(i).wait()
        return 0

    lax.fori_loop(0, CHUNKS * turns, end, 0)


def final_call(heads, group, scale, q, states, gots, pieces):
    tokens, features = q.shape
    args = [q, *[s[0] for s in states], *[s[1] for s in states], *gots, *pieces]
    vmem = pl.BlockSpec(memory_space=VMEM)
    specs = [vmem] * len(args)
    args = [near_core(x) for x in args]
    pairs = tokens * sum(x.shape[0] for x in pieces) // 2 * heads * CHUNKS
    return pl.pallas_call(
        lambda *refs: final_kernel(heads, group, scale, len(pieces), *refs),
        in_specs=specs,
        out_specs=pl.BlockSpec(memory_space=pltpu.MemorySpace.HBM),
        out_shape=jax.ShapeDtypeStruct((tokens, features), q.dtype),
        scratch_shapes=[
            pltpu.VMEM((4 * padded(heads), tokens), jnp.float32),
            pltpu.VMEM((tokens, features), q.dtype),
            pltpu.SemaphoreType.DMA((CHUNKS * heads // group,)),
        ],
        cost_estimate=pl.CostEstimate(
            flops=6 * pairs * HD,
            bytes_accessed=16 * tokens * heads * HD * 2,
            transcendentals=pairs,
        ),
        compiler_params=pltpu.CompilerParams(vmem_limit_bytes=GRANT),
        name="final",
    )(*args)


def copy_all(pairs, sems):
    copies = [pltpu.make_async_copy(x, y, sems.at[i]) for i, (x, y) in enumerate(pairs)]
    for copy in copies:
        copy.start()
    return copies


def part(c, wide):
    return slice(c * wide, (c + 1) * wide)


def sink_kernel(rows, wide, info, k, v, cand, near, sems):
    tokens = k.shape[0]
    at = pl.ds(pl.multiple_of(info[0] * rows, rows), rows)
    pairs = [(k.at[at], cand.at[:rows]), (v.at[at], cand.at[rows:])]
    pairs += [(k.at[:, :wide], near.at[:tokens]), (v.at[:, :wide], near.at[tokens:])]
    for copy in copy_all(pairs, sems):
        copy.wait()


def later_kernel(wide, band_total, width_tiles, col_count, mask, info, q, k, v, *refs):
    near, later = refs[: CHUNKS - 1], refs[CHUNKS - 1 : 2 * CHUNKS - 1]
    own, sems = refs[2 * CHUNKS - 1 :]
    tokens = q.shape[0]
    pairs = [(q.at[:, part(c, wide)], later[c].at[:, :wide]) for c in range(CHUNKS)]
    for c in range(1, CHUNKS):
        pairs += [(k.at[:, part(c, wide)], near[c - 1].at[:tokens])]
        pairs += [(v.at[:, part(c, wide)], near[c - 1].at[tokens:])]
    copies = copy_all(pairs, sems)

    band = info[1]
    core = 1 - 2 * lax.rem(band, 2)
    lane = lax.broadcasted_iota(jnp.int32, (tokens, AUX), 1)
    token = lax.broadcasted_iota(jnp.int32, (tokens, AUX), 0)
    tile = lax.rem(token, col_count) // TC
    for slot in range(2):
        full = jnp.zeros((tokens, AUX), jnp.float32)
        for j, dh in enumerate((0, core, -core)):
            inside = (band + dh >= 0) & (band + dh < band_total)
            for cq in range(width_tiles):
                for ck in range(max(0, cq - 1), min(width_tiles, cq + 2)):
                    code = slot * 9 + (dh + 1) * 3 + ck - cq + 1
                    kept = mask[0, 0, cq, code] > 0
                    if slot == 1 and j == 0 and ck == cq:
                        kept = True
                    value = jnp.where(inside & kept, 1.0, 0.0)
                    hit = (lane == j * width_tiles + ck) & (tile == cq)
                    full = jnp.where(hit, value, full)
        full = full.astype(jnp.bfloat16)
        if slot == 1:
            own[...] = full
        else:
            for c in range(CHUNKS):
                later[c][:, wide:] = full
    for copy in copies:
        copy.wait()


def prepare(q, k, v, mask, info, wide, rows, bands, col_count):
    tokens, features = q.shape
    hbm = pl.BlockSpec(memory_space=pltpu.MemorySpace.HBM)
    smem = pl.BlockSpec(memory_space=pltpu.SMEM)
    vmem = pl.BlockSpec(memory_space=VMEM)
    q, k, v = (pltpu.with_memory_space_constraint(x, pltpu.MemorySpace.HBM) for x in (q, k, v))
    params = pltpu.CompilerParams(vmem_limit_bytes=GRANT)
    near_shape = pltpu.VMEM((2 * tokens, wide), q.dtype)
    cand, near0 = pl.pallas_call(
        lambda *refs: sink_kernel(rows, wide, *refs),
        in_specs=[smem, hbm, hbm],
        out_specs=[vmem] * 2,
        out_shape=[pltpu.VMEM((2 * rows, features), q.dtype), near_shape],
        scratch_shapes=[pltpu.SemaphoreType.DMA((4,))],
        cost_estimate=pl.CostEstimate(
            flops=0, bytes_accessed=8 * tokens * wide, transcendentals=0
        ),
        compiler_params=params,
        name="sink",
    )(info, k, v)
    shapes = [near_shape] * (CHUNKS - 1)
    shapes += [pltpu.VMEM((tokens, wide + AUX), q.dtype)] * CHUNKS
    shapes.append(pltpu.VMEM((tokens, AUX), q.dtype))
    made = pl.pallas_call(
        lambda *refs: later_kernel(wide, bands, mask.shape[2], col_count, *refs),
        in_specs=[smem, smem, hbm, hbm, hbm],
        out_specs=[vmem] * len(shapes),
        out_shape=shapes,
        scratch_shapes=[pltpu.SemaphoreType.DMA((3 * CHUNKS - 2,))],
        cost_estimate=pl.CostEstimate(
            flops=0, bytes_accessed=12 * tokens * features, transcendentals=0
        ),
        compiler_params=params,
        name="later",
    )(mask, info, q, k, v)
    return cand, [near0, *made[: CHUNKS - 1]], made[CHUNKS - 1 : -1], made[-1]


def choose(mine, other, info, bit):
    def body(info, x, y, out):
        @pl.when(info[2] < bit)
        def _():
            out[...] = x[...]

        @pl.when(info[2] >= bit)
        def _():
            out[...] = y[...]

    vmem = pl.BlockSpec(memory_space=VMEM)
    return pl.pallas_call(
        body,
        in_specs=[pl.BlockSpec(memory_space=pltpu.SMEM), vmem, vmem],
        out_specs=vmem,
        out_shape=pltpu.VMEM(mine.shape, mine.dtype),
        cost_estimate=pl.CostEstimate(flops=0, bytes_accessed=4 * mine.size, transcendentals=0),
        compiler_params=pltpu.CompilerParams(vmem_limit_bytes=GRANT),
        name="choose",
    )(info, near_core(mine), near_core(other))


def swap(x, axis, bit):
    count = lax.axis_size(axis)
    return lax.ppermute(x, axis, [(i, i ^ bit) for i in range(count)])


def shards(queries, keys, values, tile_mask, sink_frame):
    frames, row_count, col_count, features = queries.shape
    tokens = frames * row_count * col_count
    head_count = features // HD
    scale = math.log2(math.e) / math.sqrt(HD)
    times, bands = lax.axis_size("tm"), lax.axis_size("height")
    t, h = lax.axis_index("tm"), lax.axis_index("height")
    assert frames == TF and col_count == 2 * TC and tile_mask.shape[:2] == (1, 1) and head_count % CHUNKS == 0
    assert times & (times - 1) == 0 and bands & (bands - 1) == 0 and bands > 1
    heads = head_count // CHUNKS
    wide = heads * HD
    group = heads

    q, k, v = (x.reshape(tokens, features) for x in (queries, keys, values))

    owner, local = sink_frame[0] // frames, sink_frame[0] % frames
    rows = row_count * col_count
    info = jnp.stack((local, h, t ^ owner)).astype(jnp.int32)
    cand, near_sent, q_sent, flags_own = prepare(
        q, k, v, tile_mask, info, wide, rows, bands, col_count
    )

    odd = [(i, i + 1) for i in range(1, bands - 1, 2)]
    odd += [(j, i) for i, j in odd]
    sooner = [(i + 1, i) for i in range(times - 1)]
    near = [lax.ppermute(x, "height", odd) for x in near_sent]
    core_k, core_v = swap(k, "height", 1), swap(v, "height", 1)
    q_later = [lax.ppermute(x, "tm", sooner) for x in q_sent]

    bit = 1
    while bit < times:
        other = swap(cand, "tm", bit)
        cand = choose(cand, other, info, bit)
        bit *= 2
    pieces = [cand]
    bit = 2
    while bit < bands:
        pieces += [swap(x, "height", bit) for x in pieces]
        bit *= 2
    twins = [swap(x, "height", 1) for x in pieces]

    states, got = [], []
    for c in range(CHUNKS):
        bands_c = [(k, 0, v, 0, False), (core_k, 0, core_v, 0, False), (near[c], 0, near[c], 1, True)]
        (pay,) = attend(c, heads, group, scale, q_later[c], None, bands_c)
        got.append(lax.ppermute(pay, "tm", [(j, i) for i, j in sooner]))
        states.append(attend(c, heads, group, scale, q, flags_own, bands_c))
    out = final_call(heads, group, scale, q, states, got, pieces + twins)
    return out.reshape(queries.shape)


def solution(mesh):
    spec = P("tm", "height", None, None)
    return jax.shard_map(
        shards,
        mesh=mesh,
        in_specs=(spec, spec, spec, spec, P()),
        out_specs=spec,
        check_vma=False,
    )
```

time: 97.7 us -> 85.4 us (0.87)
  the two profiles are of different devices: /device:TPU:1 before, /device:TPU:0 now
where the time goes in v1:
time: 85.4 us; the launch traced here: 84.9 us
  waiting for transfers between devices  46.4 us (54%)
  starting transfers between devices  21.9 us (26%)
  Pallas kernels  15.6 us (18%)
  between operations  0.89 us (1%)
    ppermute x11, waiting for transfers between devices, swap(): return lax.ppermute(x, axis, [(i, i ^ bit) for i in range(count)])  39.4 us
    ppermute x11, starting transfers between devices, swap(): return lax.ppermute(x, axis, [(i, i ^ bit) for i in range(count)])  9.78 us
    pallas_call x4, Pallas kernels, attend(): pl.pallas_call(lambda *refs: attend_kernel(chunk, heads, group, scale, pl...  8.25 us
    ppermute x2, starting transfers between devices, shards(): got.append(lax.ppermute(pay, 'tm', [(j, i) for i, j in sooner]))  8.18 us
    ppermute x2, waiting for transfers between devices, shards(): got.append(lax.ppermute(pay, 'tm', [(j, i) for i, j in sooner]))  4.55 us
    ppermute x2, starting transfers between devices, shards(): q_later = [lax.ppermute(x, 'tm', sooner) for x in q_sent]  2.57 us
    pallas_call x1, Pallas kernels, final_call(): pl.pallas_call(lambda *refs: final_kernel(heads, group, scale, len(pieces...  2.5 us
    ppermute x2, waiting for transfers between devices, shards(): q_later = [lax.ppermute(x, 'tm', sooner) for x in q_sent]  2.44 us
  transfers between devices with their start and end apart: 17, of which 5 were waited for; matrix products, arithmetic and copies ran while one was open for 0% of the time, Pallas kernels for 13%

profile of v1, /device:TPU:0, one launch (start us, length us, event | category | flops | bytes accessed | tf_op | source)
XLA Modules:
  0.0 84.9 jit_solution(16445292429386624547)
XLA Ops:
  0.8 1.8 %sink.1 = (bf16[64,2560]{1,0:T(8,128)(2,1)S(1)}, bf16[256,1280]{1,0:T(8,128)(2,1)S(1)}) custom-call(s32[3]{0:T(128)S(1)} %pad_add_fusion.refs_1_.refs_0_.info, bf16[128,2560]{1,0:T(8,128)(2,1)} %bitcast.5.refs_3_.refs_1_.refs_2_, bf16[128,2560]{1,0:T(8,128)(2,1)} %bitcast.12), custom_call_target="tpu_custom_call" | custom-call | bytes 1310720 | tf_op jit(solution)/shard_map/sink/pallas_call | solution.py:273
  2.6 3.1 %collective-permute-start.8 = (bf16[64,2560]{1,0:T(8,128)(2,1)S(1)}, bf16[64,2560]{1,0:T(8,128)(2,1)S(1)}, u32[]{:S(2)}, u32[]{:S(2)}) collective-permute-start(bf16[64,2560]{1,0:T(8,128)(2,1)S(1)} %get-tuple-element.24.x), channel_id=1, source_target_pairs={{0,8},{8,0},{16,24},{24,16},{1,9},{9,1},{17,25},{25,17},{2,10},{10... | collective-permute-start | bytes 983048 | tf_op jit(solution)/shard_map/ppermute | solution.py:327
  5.7 7.7 %collective-permute-done.8.y = bf16[64,2560]{1,0:T(8,128)(2,1)S(1)} collective-permute-done((bf16[64,2560]{1,0:T(8,128)(2,1)S(1)}, bf16[64,2560]{1,0:T(8,128)(2,1)S(1)}, u32[]{:S(2)}, u32[]{:S(2)}) %collective-permute-start.8) | collective-permute-done | bytes 327712 | tf_op jit(solution)/shard_map/ppermute | solution.py:327
  13.4 0.6 choose.2.x
  14.0 2.8 %collective-permute-start.9 = (bf16[64,2560]{1,0:T(8,128)(2,1)S(1)}, bf16[64,2560]{1,0:T(8,128)(2,1)S(1)}, u32[]{:S(2)}, u32[]{:S(2)}) collective-permute-start(bf16[64,2560]{1,0:T(8,128)(2,1)S(1)} %choose.2.x), channel_id=1, source_target_pairs={{0,16},{8,24},{16,0},{24,8},{1,17},{9,25},{17,1},{25,9},{2,18},{10... | collective-permute-start | bytes 983048 | tf_op jit(solution)/shard_map/ppermute | solution.py:327
  16.8 1.9 %later.1 = (bf16[256,1280]{1,0:T(8,128)(2,1)S(1)}, bf16[128,1408]{1,0:T(8,128)(2,1)S(1)}, bf16[128,1408]{1,0:T(8,128)(2,1)S(1)}, bf16[128,128]{1,0:T(8,128)(2,1)S(1)}) custom-call(s32[1,1,2,18]{3,2,1,0:T(2,128)S(1)} %copy-done.2, s32[3]{0:T(128)S(1)} %pad_add_fusion.refs_1_.refs_0_.info, bf16[128,2560]{1,0:T(8,128)(2,1)} %bitcast.19, ...), custom_call_target="tpu_custom_call" | custom-call | bytes 3932160 | tf_op jit(solution)/shard_map/later/pallas_call | solution.py:288
  18.7 1.3 %collective-permute-start.4 = (bf16[128,1408]{1,0:T(8,128)(2,1)S(1)}, bf16[128,1408]{1,0:T(8,128)(2,1)S(1)}, u32[]{:S(2)}, u32[]{:S(2)}) collective-permute-start(bf16[128,1408]{1,0:T(8,128)(2,1)S(1)} %get-tuple-element.22), channel_id=1, source_target_pairs={{8,0},{16,8},{24,16},{9,1},{17,9},{25,17},{10,2},{18,10},{26,18},{... | collective-permute-start | bytes 1081352 | tf_op jit(solution)/shard_map/ppermute | solution.py:357
  20.1 0.7 collective-permute-start.2
  20.8 11.1 %collective-permute-done.9.y = bf16[64,2560]{1,0:T(8,128)(2,1)S(1)} collective-permute-done((bf16[64,2560]{1,0:T(8,128)(2,1)S(1)}, bf16[64,2560]{1,0:T(8,128)(2,1)S(1)}, u32[]{:S(2)}, u32[]{:S(2)}) %collective-permute-start.9) | collective-permute-done | bytes 327712 | tf_op jit(solution)/shard_map/ppermute | solution.py:327
  31.9 0.7 collective-permute-start.3
  32.6 0.6 choose.3.refs_7_
  33.2 2.4 %collective-permute-done.4.refs_0_ = bf16[128,1408]{1,0:T(8,128)(2,1)S(1)} collective-permute-done((bf16[128,1408]{1,0:T(8,128)(2,1)S(1)}, bf16[128,1408]{1,0:T(8,128)(2,1)S(1)}, u32[]{:S(2)}, u32[]{:S(2)}) %collective-permute-start.4) | collective-permute-done | bytes 360480 | tf_op jit(solution)/shard_map/ppermute | solution.py:357
  35.6 1.4 %collective-permute-start.10 = (bf16[64,2560]{1,0:T(8,128)(2,1)S(1)}, bf16[64,2560]{1,0:T(8,128)(2,1)S(1)}, u32[]{:S(2)}, u32[]{:S(2)}) collective-permute-start(bf16[64,2560]{1,0:T(8,128)(2,1)S(1)} %choose.3.refs_7_), channel_id=1, source_target_pairs={{0,2},{1,3},{2,0},{3,1},{4,6},{5,7},{6,4},{7,5},{8,10},{9,11},{10,... | collective-permute-start | bytes 983048 | tf_op jit(solution)/shard_map/ppermute | solution.py:327
  37.0 1.3 %collective-permute-start.6 = (bf16[128,1408]{1,0:T(8,128)(2,1)S(1)}, bf16[128,1408]{1,0:T(8,128)(2,1)S(1)}, u32[]{:S(2)}, u32[]{:S(2)}) collective-permute-start(bf16[128,1408]{1,0:T(8,128)(2,1)S(1)} %get-tuple-element.23), channel_id=1, source_target_pairs={{8,0},{16,8},{24,16},{9,1},{17,9},{25,17},{10,2},{18,10},{26,18},{... | collective-permute-start | bytes 1081352 | tf_op jit(solution)/shard_map/ppermute | solution.py:357
  38.3 1.6 %collective-permute-start.11 = (bf16[64,2560]{1,0:T(8,128)(2,1)S(1)}, bf16[64,2560]{1,0:T(8,128)(2,1)S(1)}, u32[]{:S(2)}, u32[]{:S(2)}) collective-permute-start(bf16[64,2560]{1,0:T(8,128)(2,1)S(1)} %choose.3.refs_7_), channel_id=1, source_target_pairs={{0,4},{1,5},{2,6},{3,7},{4,0},{5,1},{6,2},{7,3},{8,12},{9,13},{10,... | collective-permute-start | bytes 983048 | tf_op jit(solution)/shard_map/ppermute | solution.py:327
  39.9 20.5 %collective-permute-done.10.refs_8_ = bf16[64,2560]{1,0:T(8,128)(2,1)S(1)} collective-permute-done((bf16[64,2560]{1,0:T(8,128)(2,1)S(1)}, bf16[64,2560]{1,0:T(8,128)(2,1)S(1)}, u32[]{:S(2)}, u32[]{:S(2)}) %collective-permute-start.10) | collective-permute-done | bytes 327712 | tf_op jit(solution)/shard_map/ppermute | solution.py:327
  60.6 2.1 %attend.6 = bf16[1360,128]{1,0:T(8,128)(2,1)S(1)} custom-call(bf16[128,1408]{1,0:T(8,128)(2,1)S(1)} %collective-permute-done.4.refs_0_, bf16[128,2560]{1,0:T(8,128)(2,1)} %bitcast.5.refs_3_.refs_1_.refs_2_, bf16[128,2560]{1,0:T(8,128)(2,1)S(1)} %bitcast.15, bf16[128,2560]{1,0:T(8,128)(2,1)S(1)} %collective-permute-done.refs_4_.refs_3_, ...), custom_call_target="tpu_custom_call" | custom-call | flops 377487360 | bytes 3276800 | tf_op jit(solution)/shard_map/attend/pallas_call | solution.py:110
  62.7 4.7 %collective-permute-start.5 = (bf16[1360,128]{1,0:T(8,128)(2,1)S(1)}, bf16[1360,128]{1,0:T(8,128)(2,1)S(1)}, u32[]{:S(2)}, u32[]{:S(2)}) collective-permute-start(bf16[1360,128]{1,0:T(8,128)(2,1)S(1)} %attend.6), channel_id=1, source_target_pairs={{0,8},{8,16},{16,24},{1,9},{9,17},{17,25},{2,10},{10,18},{18,26},{... | collective-permute-start | bytes 1044488 | tf_op jit(solution)/shard_map/ppermute | solution.py:375
  67.4 2.1 %attend.7 = bf16[1360,128]{1,0:T(8,128)(2,1)S(1)} custom-call(bf16[128,1408]{1,0:T(8,128)(2,1)S(1)} %collective-permute-done.6.refs_0_, bf16[128,2560]{1,0:T(8,128)(2,1)} %bitcast.5.refs_3_.refs_1_.refs_2_, bf16[128,2560]{1,0:T(8,128)(2,1)S(1)} %bitcast.16, bf16[128,2560]{1,0:T(8,128)(2,1)S(1)} %collective-permute-done.refs_4_.refs_3_, ...), custom_call_target="tpu_custom_call" | custom-call | flops 377487360 | bytes 3276800 | tf_op jit(solution)/shard_map/attend/pallas_call | solution.py:110
  69.5 3.5 %collective-permute-start.7 = (bf16[1360,128]{1,0:T(8,128)(2,1)S(1)}, bf16[1360,128]{1,0:T(8,128)(2,1)S(1)}, u32[]{:S(2)}, u32[]{:S(2)}) collective-permute-start(bf16[1360,128]{1,0:T(8,128)(2,1)S(1)} %attend.7), channel_id=1, source_target_pairs={{0,8},{8,16},{16,24},{1,9},{9,17},{17,25},{2,10},{10,18},{18,26},{... | collective-permute-start | bytes 1044488 | tf_op jit(solution)/shard_map/ppermute | solution.py:375
  73.7 2.1 %attend.4 = (f32[1280,128]{1,0:T(8,128)S(1)}, f32[32,128]{1,0:T(8,128)S(1)}) custom-call(bf16[128,2560]{1,0:T(8,128)(2,1)S(1)} %bitcast.20, bf16[128,128]{1,0:T(8,128)(2,1)S(1)} %get-tuple-element.15.refs_1_, bf16[128,2560]{1,0:T(8,128)(2,1)} %bitcast.5.refs_3_.refs_1_.refs_2_, bf16[128,2560]{1,0:T(8,128)(2,1)S(1)} %bitcast.17, ...), custom_call_target="tpu_custom_call" | custom-call | flops 377487360 | bytes 3276800 | tf_op jit(solution)/shard_map/attend/pallas_call | solution.py:110
  75.7 2.1 %attend.5 = (f32[1280,128]{1,0:T(8,128)S(1)}, f32[32,128]{1,0:T(8,128)S(1)}) custom-call(bf16[128,2560]{1,0:T(8,128)(2,1)S(1)} %bitcast.21, bf16[128,128]{1,0:T(8,128)(2,1)S(1)} %get-tuple-element.15.refs_1_, bf16[128,2560]{1,0:T(8,128)(2,1)} %bitcast.5.refs_3_.refs_1_.refs_2_, bf16[128,2560]{1,0:T(8,128)(2,1)S(1)} %bitcast.18, ...), custom_call_target="tpu_custom_call" | custom-call | flops 377487360 | bytes 3276800 | tf_op jit(solution)/shard_map/attend/pallas_call | solution.py:110
  77.8 4.5 %collective-permute-done.7.refs_6_ = bf16[1360,128]{1,0:T(8,128)(2,1)S(1)} collective-permute-done((bf16[1360,128]{1,0:T(8,128)(2,1)S(1)}, bf16[1360,128]{1,0:T(8,128)(2,1)S(1)}, u32[]{:S(2)}, u32[]{:S(2)}) %collective-permute-start.7) | collective-permute-done | bytes 348192 | tf_op jit(solution)/shard_map/ppermute | solution.py:375
  82.4 2.5 %final.1 = bf16[128,2560]{1,0:T(8,128)(2,1)} custom-call(bf16[128,2560]{1,0:T(8,128)(2,1)S(1)} %bitcast.22, f32[1280,128]{1,0:T(8,128)S(1)} %get-tuple-element.17.refs_1_, f32[1280,128]{1,0:T(8,128)S(1)} %get-tuple-element.19.refs_2_, f32[32,128]{1,0:T(8,128)S(1)} %get-tuple-element.20.refs_3_, f32[32,128]{1,0:T(8,128)S(1)} %get-tuple-element.21.refs_4_, ...), custom_call_target="tpu_custom_call" | custom-call | flops 503316480 | bytes 5242880 | tf_op jit(solution)/shard_map/final/pallas_call | solution.py:187
  (26 shorter events, 1.0 us)
Async XLA Ops:
  2.6 10.8 %collective-permute-start.8 = (bf16[64,2560]{1,0:T(8,128)(2,1)S(1)}, bf16[64,2560]{1,0:T(8,128)(2,1)S(1)}, u32[]{:S(2)}, u32[]{:S(2)}) collective-permute-start(bf16[64,2560]{1,0:T(8,128)(2,1)S(1)} %get-tuple-element.24.x), channel_id=1, source_target_pairs={{0,8},{8,0},{16,24},{24,16},{1,9},{9,1},{17,25},{25,17},{2,10},{10... | collective-permute-start | bytes 983048 | tf_op jit(solution)/shard_map/ppermute | solution.py:327
  5.7 31.3 %collective-permute-start = (bf16[128,2560]{1,0:T(8,128)(2,1)}, bf16[128,2560]{1,0:T(8,128)(2,1)S(1)}, u32[]{:S(2)}, u32[]{:S(2)}) collective-permute-start(bf16[128,2560]{1,0:T(8,128)(2,1)} %bitcast.5.refs_3_.refs_1_.refs_2_), channel_id=1, source_target_pairs={{0,1},{1,0},{2,3},{3,2},{4,5},{5,4},{6,7},{7,6},{8,9},{9,8},{10,11... | collective-permute-start | bytes 1966088 | tf_op jit(solution)/shard_map/ppermute | solution.py:327
  14.0 2.8 %copy-start.2 = (s32[1,1,2,18]{3,2,1,0:T(2,128)S(1)}, s32[1,1,2,18]{3,2,1,0:T(2,128)}, u32[]{:S(2)}) copy-start(s32[1,1,2,18]{3,2,1,0:T(2,128)} %refs_0_.1) | copy-start | bytes 436
  14.0 17.9 %collective-permute-start.9 = (bf16[64,2560]{1,0:T(8,128)(2,1)S(1)}, bf16[64,2560]{1,0:T(8,128)(2,1)S(1)}, u32[]{:S(2)}, u32[]{:S(2)}) collective-permute-start(bf16[64,2560]{1,0:T(8,128)(2,1)S(1)} %choose.2.x), channel_id=1, source_target_pairs={{0,16},{8,24},{16,0},{24,8},{1,17},{9,25},{17,1},{25,9},{2,18},{10... | collective-permute-start | bytes 983048 | tf_op jit(solution)/shard_map/ppermute | solution.py:327
  16.8 3.2 %copy-start = (bf16[4,2,16,2560]{3,2,1,0:T(8,128)(2,1)S(1)}, bf16[4,2,16,2560]{3,2,1,0:T(8,128)(2,1)}, u32[]{:S(2)}) copy-start(bf16[4,2,16,2560]{3,2,1,0:T(8,128)(2,1)} %param.7) | copy-start | bytes 1966084
  18.7 16.9 %collective-permute-start.4 = (bf16[128,1408]{1,0:T(8,128)(2,1)S(1)}, bf16[128,1408]{1,0:T(8,128)(2,1)S(1)}, u32[]{:S(2)}, u32[]{:S(2)}) collective-permute-start(bf16[128,1408]{1,0:T(8,128)(2,1)S(1)} %get-tuple-element.22), channel_id=1, source_target_pairs={{8,0},{16,8},{24,16},{9,1},{17,9},{25,17},{10,2},{18,10},{26,18},{... | collective-permute-start | bytes 1081352 | tf_op jit(solution)/shard_map/ppermute | solution.py:357
  20.0 18.3 %collective-permute-start.1 = (bf16[128,2560]{1,0:T(8,128)(2,1)S(1)}, bf16[128,2560]{1,0:T(8,128)(2,1)S(1)}, u32[]{:S(2)}, u32[]{:S(2)}) collective-permute-start(bf16[128,2560]{1,0:T(8,128)(2,1)S(1)} %bitcast.14), channel_id=1, source_target_pairs={{0,1},{1,0},{2,3},{3,2},{4,5},{5,4},{6,7},{7,6},{8,9},{9,8},{10,11... | collective-permute-start | bytes 1966088 | tf_op jit(solution)/shard_map/ppermute | solution.py:327
  20.1 19.8 %collective-permute-start.2 = (bf16[256,1280]{1,0:T(8,128)(2,1)S(1)}, bf16[256,1280]{1,0:T(8,128)(2,1)S(1)}, u32[]{:S(2)}, u32[]{:S(2)}) collective-permute-start(bf16[256,1280]{1,0:T(8,128)(2,1)S(1)} %get-tuple-element.16), channel_id=1, source_target_pairs={{1,2},{3,4},{5,6},{2,1},{4,3},{6,5},{9,10},{11,12},{13,14},{10,9},... | collective-permute-start | bytes 1966088 | tf_op jit(solution)/shard_map/ppermute | solution.py:355
  31.9 35.5 %collective-permute-start.3 = (bf16[256,1280]{1,0:T(8,128)(2,1)S(1)}, bf16[256,1280]{1,0:T(8,128)(2,1)S(1)}, u32[]{:S(2)}, u32[]{:S(2)}) collective-permute-start(bf16[256,1280]{1,0:T(8,128)(2,1)S(1)} %get-tuple-element.18), channel_id=1, source_target_pairs={{1,2},{3,4},{5,6},{2,1},{4,3},{6,5},{9,10},{11,12},{13,14},{10,9},... | collective-permute-start | bytes 1966088 | tf_op jit(solution)/shard_map/ppermute | solution.py:355
  35.6 24.8 %collective-permute-start.10 = (bf16[64,2560]{1,0:T(8,128)(2,1)S(1)}, bf16[64,2560]{1,0:T(8,128)(2,1)S(1)}, u32[]{:S(2)}, u32[]{:S(2)}) collective-permute-start(bf16[64,2560]{1,0:T(8,128)(2,1)S(1)} %choose.3.refs_7_), channel_id=1, source_target_pairs={{0,2},{1,3},{2,0},{3,1},{4,6},{5,7},{6,4},{7,5},{8,10},{9,11},{10,... | collective-permute-start | bytes 983048 | tf_op jit(solution)/shard_map/ppermute | solution.py:327
  37.0 25.7 %collective-permute-start.6 = (bf16[128,1408]{1,0:T(8,128)(2,1)S(1)}, bf16[128,1408]{1,0:T(8,128)(2,1)S(1)}, u32[]{:S(2)}, u32[]{:S(2)}) collective-permute-start(bf16[128,1408]{1,0:T(8,128)(2,1)S(1)} %get-tuple-element.23), channel_id=1, source_target_pairs={{8,0},{16,8},{24,16},{9,1},{17,9},{25,17},{10,2},{18,10},{26,18},{... | collective-permute-start | bytes 1081352 | tf_op jit(solution)/shard_map/ppermute | solution.py:357
  38.3 34.7 %collective-permute-start.11 = (bf16[64,2560]{1,0:T(8,128)(2,1)S(1)}, bf16[64,2560]{1,0:T(8,128)(2,1)S(1)}, u32[]{:S(2)}, u32[]{:S(2)}) collective-permute-start(bf16[64,2560]{1,0:T(8,128)(2,1)S(1)} %choose.3.refs_7_), channel_id=1, source_target_pairs={{0,4},{1,5},{2,6},{3,7},{4,0},{5,1},{6,2},{7,3},{8,12},{9,13},{10,... | collective-permute-start | bytes 983048 | tf_op jit(solution)/shard_map/ppermute | solution.py:327
  39.9 33.2 %collective-permute-start.13 = (bf16[64,2560]{1,0:T(8,128)(2,1)S(1)}, bf16[64,2560]{1,0:T(8,128)(2,1)S(1)}, u32[]{:S(2)}, u32[]{:S(2)}) collective-permute-start(bf16[64,2560]{1,0:T(8,128)(2,1)S(1)} %choose.3.refs_7_), channel_id=1, source_target_pairs={{0,1},{1,0},{2,3},{3,2},{4,5},{5,4},{6,7},{7,6},{8,9},{9,8},{10,11... | collective-permute-start | bytes 983048 | tf_op jit(solution)/shard_map/ppermute | solution.py:327
  60.4 13.1 %collective-permute-start.12 = (bf16[64,2560]{1,0:T(8,128)(2,1)S(1)}, bf16[64,2560]{1,0:T(8,128)(2,1)S(1)}, u32[]{:S(2)}, u32[]{:S(2)}) collective-permute-start(bf16[64,2560]{1,0:T(8,128)(2,1)S(1)} %collective-permute-done.10.refs_8_), channel_id=1, source_target_pairs={{0,4},{1,5},{2,6},{3,7},{4,0},{5,1},{6,2},{7,3},{8,12},{9,13},{10,... | collective-permute-start | bytes 983048 | tf_op jit(solution)/shard_map/ppermute | solution.py:327
  62.7 11.0 %copy-start.1 = (bf16[4,2,16,2560]{3,2,1,0:T(8,128)(2,1)S(1)}, bf16[4,2,16,2560]{3,2,1,0:T(8,128)(2,1)}, u32[]{:S(2)}) copy-start(bf16[4,2,16,2560]{3,2,1,0:T(8,128)(2,1)} %param.5) | copy-start | bytes 1966084
  62.7 15.1 %collective-permute-start.5 = (bf16[1360,128]{1,0:T(8,128)(2,1)S(1)}, bf16[1360,128]{1,0:T(8,128)(2,1)S(1)}, u32[]{:S(2)}, u32[]{:S(2)}) collective-permute-start(bf16[1360,128]{1,0:T(8,128)(2,1)S(1)} %attend.6), channel_id=1, source_target_pairs={{0,8},{8,16},{16,24},{1,9},{9,17},{17,25},{2,10},{10,18},{18,26},{... | collective-permute-start | bytes 1044488 | tf_op jit(solution)/shard_map/ppermute | solution.py:375
  69.5 12.9 %collective-permute-start.7 = (bf16[1360,128]{1,0:T(8,128)(2,1)S(1)}, bf16[1360,128]{1,0:T(8,128)(2,1)S(1)}, u32[]{:S(2)}, u32[]{:S(2)}) collective-permute-start(bf16[1360,128]{1,0:T(8,128)(2,1)S(1)} %attend.7), channel_id=1, source_target_pairs={{0,8},{8,16},{16,24},{1,9},{9,17},{17,25},{2,10},{10,18},{18,26},{... | collective-permute-start | bytes 1044488 | tf_op jit(solution)/shard_map/ppermute | solution.py:375
  73.0 9.4 %collective-permute-start.14 = (bf16[64,2560]{1,0:T(8,128)(2,1)S(1)}, bf16[64,2560]{1,0:T(8,128)(2,1)S(1)}, u32[]{:S(2)}, u32[]{:S(2)}) collective-permute-start(bf16[64,2560]{1,0:T(8,128)(2,1)S(1)} %collective-permute-done.10.refs_8_), channel_id=1, source_target_pairs={{0,1},{1,0},{2,3},{3,2},{4,5},{5,4},{6,7},{7,6},{8,9},{9,8},{10,11... | collective-permute-start | bytes 983048 | tf_op jit(solution)/shard_map/ppermute | solution.py:327
  73.1 9.3 %collective-permute-start.15 = (bf16[64,2560]{1,0:T(8,128)(2,1)S(1)}, bf16[64,2560]{1,0:T(8,128)(2,1)S(1)}, u32[]{:S(2)}, u32[]{:S(2)}) collective-permute-start(bf16[64,2560]{1,0:T(8,128)(2,1)S(1)} %collective-permute-done.11.refs_9_), channel_id=1, source_target_pairs={{0,1},{1,0},{2,3},{3,2},{4,5},{5,4},{6,7},{7,6},{8,9},{9,8},{10,11... | collective-permute-start | bytes 983048 | tf_op jit(solution)/shard_map/ppermute | solution.py:327
  73.6 8.8 %collective-permute-start.16 = (bf16[64,2560]{1,0:T(8,128)(2,1)S(1)}, bf16[64,2560]{1,0:T(8,128)(2,1)S(1)}, u32[]{:S(2)}, u32[]{:S(2)}) collective-permute-start(bf16[64,2560]{1,0:T(8,128)(2,1)S(1)} %collective-permute-done.12.refs_10_), channel_id=1, source_target_pairs={{0,1},{1,0},{2,3},{3,2},{4,5},{5,4},{6,7},{7,6},{8,9},{9,8},{10,11... | collective-permute-start | bytes 983048 | tf_op jit(solution)/shard_map/ppermute | solution.py:327

commit v2 on v1

--- a/solution.py
+++ b/solution.py
@@ -121,20 +121,14 @@
     )(*[near_core(x) for x in args])
 
 
-def final_kernel(heads, group, scale, n_sink, *refs):
+def final_kernel(heads, cut, scale, n_sink, *refs):
     q = refs[0]
     accs, stats, gots = (refs[1 + i * CHUNKS :][:CHUNKS] for i in range(3))
-    pieces = refs[1 + 3 * CHUNKS : 1 + 3 * CHUNKS + n_sink]
-    rows = pieces[0].shape[0] // 2
-    out, state, done, sems = refs[-4:]
+    pieces = [refs[1 + 3 * CHUNKS + c * n_sink :][:n_sink] for c in range(CHUNKS)]
+    rows = pieces[0][0].shape[0] // 2
+    out, done, sems = refs[-3:]
     pad = padded(heads)
-    wide = group * HD
-    turns = heads // group
-
-    def copy(turn):
-        at = pl.ds(pl.multiple_of(turn * wide, HD), wide)
-        return pltpu.make_async_copy(done.at[:, at], out.at[:, at], sems.at[turn])
-
+    copies = []
     for c in range(CHUNKS):
         got = gots[c]
         part = [
@@ -146,53 +140,48 @@
         m2 = jnp.where(l2 > 0, part[0] + part[1] + part[2], NEG)
         m12 = jnp.maximum(m1, m2)
         e1, e2 = jnp.exp2(m1 - m12), jnp.exp2(m2 - m12)
-        for i, x in enumerate((m12, e1, e2, e1 * l1 + e2 * l2)):
-            state[i * pad : (i + 1) * pad] = x
-
-        def step(i, _):
-            for g in range(group):
-                head = i * group + g
-                there, here = lanes(c * heads + head), lanes(head)
-                m12, e1, e2, l12 = (state[pl.ds(n * pad + head, 1)] for n in range(4))
-                k = jnp.concatenate([r[:rows, there] for r in pieces], axis=0)
-                v = jnp.concatenate([r[rows:, there] for r in pieces], axis=0)
-                s = dot(k, q[:, there], 1) * scale
-                top = jnp.maximum(jnp.max(s, axis=0, keepdims=True), m12)
-                p = jnp.exp2(s - top).astype(jnp.bfloat16)
-                f = jnp.exp2(m12 - top)
-                den = jnp.sum(p.astype(jnp.float32), axis=0, keepdims=True) + f * l12
-                inv = 1.0 / den
-                theirs = got[here].astype(jnp.float32)
-                res = dot(v, p, 0) * inv + accs[c][here] * (f * e1 * inv) + theirs * (f * e2 * inv)
-                done[:, there] = res.T.astype(done.dtype)
-            copy(c * turns + i).start()
-            return 0
-
-        lax.fori_loop(0, turns, step, 0)
-
-    def end(i, _):
-        copy(i).wait()
-        return 0
-
-    lax.fori_loop(0, CHUNKS * turns, end, 0)
-
-
-def final_call(heads, group, scale, q, states, gots, pieces):
+        l12 = e1 * l1 + e2 * l2
+        for head in range(heads):
+            one, here = slice(head, head + 1), slice(head * HD, (head + 1) * HD)
+            at = (c * heads + head) * HD
+            there = slice(at, at + HD)
+            k = jnp.concatenate([r[:rows, here] for r in pieces[c]], axis=0)
+            v = jnp.concatenate([r[rows:, here] for r in pieces[c]], axis=0)
+            s = dot(k, q[:, there], 1) * scale
+            top = jnp.maximum(jnp.max(s, axis=0, keepdims=True), m12[one])
+            p = jnp.exp2(s - top).astype(jnp.bfloat16)
+            f = jnp.exp2(m12[one] - top)
+            inv = 1.0 / (jnp.sum(p.astype(jnp.float32), axis=0, keepdims=True) + f * l12[one])
+            theirs = got[here].astype(jnp.float32)
+            mine = accs[c][here] * (f * e1[one] * inv)
+            res = dot(v, p, 0) * inv + mine + theirs * (f * e2[one] * inv)
+            done[:, there] = res.T.astype(done.dtype)
+            if (c * heads + head + 1) % cut == 0:
+                cols = pl.ds(at + HD - cut * HD, cut * HD)
+                copies.append(
+                    pltpu.make_async_copy(done.at[:, cols], out.at[:, cols], sems.at[len(copies)])
+                )
+                copies[-1].start()
+    for copy in copies:
+        copy.wait()
+
+
+def final_call(heads, scale, q, states, gots, pieces):
     tokens, features = q.shape
-    args = [q, *[s[0] for s in states], *[s[1] for s in states], *gots, *pieces]
+    cut = math.gcd(CHUNKS * heads, 5)
+    args = [q, *[s[0] for s in states], *[s[1] for s in states], *gots, *[x for p in pieces for x in p]]
     vmem = pl.BlockSpec(memory_space=VMEM)
     specs = [vmem] * len(args)
     args = [near_core(x) for x in args]
-    pairs = tokens * sum(x.shape[0] for x in pieces) // 2 * heads * CHUNKS
+    pairs = tokens * sum(x.shape[0] for x in pieces[0]) // 2 * heads * CHUNKS
     return pl.pallas_call(
-        lambda *refs: final_kernel(heads, group, scale, len(pieces), *refs),
+        lambda *refs: final_kernel(heads, cut, scale, len(pieces[0]), *refs),
         in_specs=specs,
         out_specs=pl.BlockSpec(memory_space=pltpu.MemorySpace.HBM),
         out_shape=jax.ShapeDtypeStruct((tokens, features), q.dtype),
         scratch_shapes=[
-            pltpu.VMEM((4 * padded(heads), tokens), jnp.float32),
             pltpu.VMEM((tokens, features), q.dtype),
-            pltpu.SemaphoreType.DMA((CHUNKS * heads // group,)),
+            pltpu.SemaphoreType.DMA((CHUNKS * heads // cut,)),
         ],
         cost_estimate=pl.CostEstimate(
             flops=6 * pairs * HD,
@@ -300,22 +289,26 @@
     return cand, [near0, *made[: CHUNKS - 1]], made[CHUNKS - 1 : -1], made[-1]
 
 
-def choose(mine, other, info, bit):
-    def body(info, x, y, out):
+def choose(mine, other, info, bit, parts):
+    wide = mine.shape[1] // parts
+
+    def body(info, x, y, *outs):
         @pl.when(info[2] < bit)
         def _():
-            out[...] = x[...]
+            for i, out in enumerate(outs):
+                out[...] = x[:, part(i, wide)]
 
         @pl.when(info[2] >= bit)
         def _():
-            out[...] = y[...]
+            for i, out in enumerate(outs):
+                out[...] = y[:, part(i, wide)]
 
     vmem = pl.BlockSpec(memory_space=VMEM)
     return pl.pallas_call(
         body,
         in_specs=[pl.BlockSpec(memory_space=pltpu.SMEM), vmem, vmem],
-        out_specs=vmem,
-        out_shape=pltpu.VMEM(mine.shape, mine.dtype),
+        out_specs=[vmem] * parts,
+        out_shape=[pltpu.VMEM((mine.shape[0], wide), mine.dtype)] * parts,
         cost_estimate=pl.CostEstimate(flops=0, bytes_accessed=4 * mine.size, transcendentals=0),
         compiler_params=pltpu.CompilerParams(vmem_limit_bytes=GRANT),
         name="choose",
@@ -335,7 +328,7 @@
     times, bands = lax.axis_size("tm"), lax.axis_size("height")
     t, h = lax.axis_index("tm"), lax.axis_index("height")
     assert frames == TF and col_count == 2 * TC and tile_mask.shape[:2] == (1, 1) and head_count % CHUNKS == 0
-    assert times & (times - 1) == 0 and bands & (bands - 1) == 0 and bands > 1
+    assert times & (times - 1) == 0 and bands & (bands - 1) == 0 and min(times, bands) > 1
     heads = head_count // CHUNKS
     wide = heads * HD
     group = heads
@@ -356,17 +349,16 @@
     core_k, core_v = swap(k, "height", 1), swap(v, "height", 1)
     q_later = [lax.ppermute(x, "tm", sooner) for x in q_sent]
 
-    bit = 1
-    while bit < times:
-        other = swap(cand, "tm", bit)
-        cand = choose(cand, other, info, bit)
-        bit *= 2
-    pieces = [cand]
-    bit = 2
-    while bit < bands:
-        pieces += [swap(x, "height", bit) for x in pieces]
-        bit *= 2
-    twins = [swap(x, "height", 1) for x in pieces]
+    parts = choose(cand, swap(cand, "tm", 1), info, 1, CHUNKS)
+    pieces = []
+    for cand in parts:
+        bit = 2
+        while bit < times:
+            other = swap(cand, "tm", bit)
+            (cand,) = choose(cand, other, info, bit, 1)
+            bit *= 2
+        mine = [cand] + [swap(cand, "height", d) for d in range(2, bands, 2)]
+        pieces.append(mine + [swap(x, "height", 1) for x in mine])
 
     states, got = [], []
     for c in range(CHUNKS):
@@ -374,7 +366,7 @@
         (pay,) = attend(c, heads, group, scale, q_later[c], None, bands_c)
         got.append(lax.ppermute(pay, "tm", [(j, i) for i, j in sooner]))
         states.append(attend(c, heads, group, scale, q, flags_own, bands_c))
-    out = final_call(heads, group, scale, q, states, got, pieces + twins)
+    out = final_call(heads, scale, q, states, got, pieces)
     return out.reshape(queries.shape)
 
 

time: 85.4 us -> 88.5 us (1.036)
  the two profiles are of different devices: /device:TPU:0 before, /device:TPU:18 now
where the time goes in v2:
time: 88.5 us; the launch traced here: 88.2 us
  waiting for transfers between devices  45.1 us (51%)
  starting transfers between devices  29.7 us (34%)
  Pallas kernels  11.6 us (13%)
  between operations  0.95 us (1%)
    ppermute x19, waiting for transfers between devices, swap(): return lax.ppermute(x, axis, [(i, i ^ bit) for i in range(count)])  29.3 us
    ppermute x19, starting transfers between devices, swap(): return lax.ppermute(x, axis, [(i, i ^ bit) for i in range(count)])  15.9 us
    ppermute x2, waiting for transfers between devices, shards(): got.append(lax.ppermute(pay, 'tm', [(j, i) for i, j in sooner]))  11.4 us
    ppermute x2, starting transfers between devices, shards(): near = [lax.ppermute(x, 'height', odd) for x in near_sent]  5.55 us
    ppermute x2, starting transfers between devices, shards(): q_later = [lax.ppermute(x, 'tm', sooner) for x in q_sent]  4.4 us
    ppermute x2, waiting for transfers between devices, shards(): near = [lax.ppermute(x, 'height', odd) for x in near_sent]  4.01 us
    pallas_call x4, Pallas kernels, attend(): pl.pallas_call(lambda *refs: attend_kernel(chunk, heads, group, scale, pl...  3.86 us
    ppermute x2, starting transfers between devices, shards(): got.append(lax.ppermute(pay, 'tm', [(j, i) for i, j in sooner]))  3.84 us
  transfers between devices with their start and end apart: 25, of which 11 were waited for; matrix products, arithmetic and copies ran while one was open for 0% of the time, Pallas kernels for 8%

profile of v2, /device:TPU:18, one launch (start us, length us, event | category | flops | bytes accessed | tf_op | source)
XLA Modules:
  0.0 88.2 jit_solution(2257901364698310897)
XLA Ops:
  1.4 1.9 %later.1 = (bf16[256,1280]{1,0:T(8,128)(2,1)S(1)}, bf16[128,1408]{1,0:T(8,128)(2,1)S(1)}, bf16[128,1408]{1,0:T(8,128)(2,1)S(1)}, bf16[128,128]{1,0:T(8,128)(2,1)S(1)}) custom-call(s32[1,1,2,18]{3,2,1,0:T(2,128)S(1)} %copy-done.3, s32[3]{0:T(128)S(1)} %pad_add_fusion.refs_1_.refs_0_.info, bf16[128,2560]{1,0:T(8,128)(2,1)} %bitcast.26, ...), custom_call_target="tpu_custom_call" | custom-call | bytes 3932160 | tf_op jit(solution)/shard_map/later/pallas_call | solution.py:277
  3.3 2.5 %collective-permute-start.4 = (bf16[128,1408]{1,0:T(8,128)(2,1)S(1)}, bf16[128,1408]{1,0:T(8,128)(2,1)S(1)}, u32[]{:S(2)}, u32[]{:S(2)}) collective-permute-start(bf16[128,1408]{1,0:T(8,128)(2,1)S(1)} %get-tuple-element.24), channel_id=1, source_target_pairs={{8,0},{16,8},{24,16},{9,1},{17,9},{25,17},{10,2},{18,10},{26,18},{... | collective-permute-start | bytes 1081352 | tf_op jit(solution)/shard_map/ppermute | solution.py:350
  5.8 1.8 %sink.1 = (bf16[64,2560]{1,0:T(8,128)(2,1)S(1)}, bf16[256,1280]{1,0:T(8,128)(2,1)S(1)}) custom-call(s32[3]{0:T(128)S(1)} %pad_add_fusion.refs_1_.refs_0_.info, bf16[128,2560]{1,0:T(8,128)(2,1)} %bitcast.13, bf16[128,2560]{1,0:T(8,128)(2,1)} %bitcast.20), custom_call_target="tpu_custom_call" | custom-call | bytes 1310720 | tf_op jit(solution)/shard_map/sink/pallas_call | solution.py:262
  7.6 1.7 %collective-permute-start.8 = (bf16[64,2560]{1,0:T(8,128)(2,1)S(1)}, bf16[64,2560]{1,0:T(8,128)(2,1)S(1)}, u32[]{:S(2)}, u32[]{:S(2)}) collective-permute-start(bf16[64,2560]{1,0:T(8,128)(2,1)S(1)} %get-tuple-element.26.x), channel_id=1, source_target_pairs={{0,8},{8,0},{16,24},{24,16},{1,9},{9,1},{17,25},{25,17},{2,10},{10... | collective-permute-start | bytes 983048 | tf_op jit(solution)/shard_map/ppermute | solution.py:320
  9.3 1.9 %collective-permute-start.6 = (bf16[128,1408]{1,0:T(8,128)(2,1)S(1)}, bf16[128,1408]{1,0:T(8,128)(2,1)S(1)}, u32[]{:S(2)}, u32[]{:S(2)}) collective-permute-start(bf16[128,1408]{1,0:T(8,128)(2,1)S(1)} %get-tuple-element.25), channel_id=1, source_target_pairs={{8,0},{16,8},{24,16},{9,1},{17,9},{25,17},{10,2},{18,10},{26,18},{... | collective-permute-start | bytes 1081352 | tf_op jit(solution)/shard_map/ppermute | solution.py:350
  11.8 11.8 %collective-permute-done.8.y = bf16[64,2560]{1,0:T(8,128)(2,1)S(1)} collective-permute-done((bf16[64,2560]{1,0:T(8,128)(2,1)S(1)}, bf16[64,2560]{1,0:T(8,128)(2,1)S(1)}, u32[]{:S(2)}, u32[]{:S(2)}) %collective-permute-start.8) | collective-permute-done | bytes 327712 | tf_op jit(solution)/shard_map/ppermute | solution.py:320
  23.7 1.9 %collective-permute-start.2 = (bf16[256,1280]{1,0:T(8,128)(2,1)S(1)}, bf16[256,1280]{1,0:T(8,128)(2,1)S(1)}, u32[]{:S(2)}, u32[]{:S(2)}) collective-permute-start(bf16[256,1280]{1,0:T(8,128)(2,1)S(1)} %get-tuple-element.18), channel_id=1, source_target_pairs={{1,2},{3,4},{5,6},{2,1},{4,3},{6,5},{9,10},{11,12},{13,14},{10,9},... | collective-permute-start | bytes 1966088 | tf_op jit(solution)/shard_map/ppermute | solution.py:348
  25.6 3.6 %collective-permute-start.3 = (bf16[256,1280]{1,0:T(8,128)(2,1)S(1)}, bf16[256,1280]{1,0:T(8,128)(2,1)S(1)}, u32[]{:S(2)}, u32[]{:S(2)}) collective-permute-start(bf16[256,1280]{1,0:T(8,128)(2,1)S(1)} %get-tuple-element.20), channel_id=1, source_target_pairs={{1,2},{3,4},{5,6},{2,1},{4,3},{6,5},{9,10},{11,12},{13,14},{10,9},... | collective-permute-start | bytes 1966088 | tf_op jit(solution)/shard_map/ppermute | solution.py:348
  30.6 6.3 %collective-permute-done.9.y = bf16[64,1280]{1,0:T(8,128)(2,1)S(1)} collective-permute-done((bf16[64,1280]{1,0:T(8,128)(2,1)S(1)}, bf16[64,1280]{1,0:T(8,128)(2,1)S(1)}, u32[]{:S(2)}, u32[]{:S(2)}) %collective-permute-start.9) | collective-permute-done | bytes 163872 | tf_op jit(solution)/shard_map/ppermute | solution.py:320
  36.9 2.8 %collective-permute-start.17 = (bf16[64,1280]{1,0:T(8,128)(2,1)S(1)}, bf16[64,1280]{1,0:T(8,128)(2,1)S(1)}, u32[]{:S(2)}, u32[]{:S(2)}) collective-permute-start(bf16[64,1280]{1,0:T(8,128)(2,1)S(1)} %get-tuple-element.28.x), channel_id=1, source_target_pairs={{0,16},{8,24},{16,0},{24,8},{1,17},{9,25},{17,1},{25,9},{2,18},{10... | collective-permute-start | bytes 491528 | tf_op jit(solution)/shard_map/ppermute | solution.py:320
  40.2 5.1 %collective-permute-done.17.y = bf16[64,1280]{1,0:T(8,128)(2,1)S(1)} collective-permute-done((bf16[64,1280]{1,0:T(8,128)(2,1)S(1)}, bf16[64,1280]{1,0:T(8,128)(2,1)S(1)}, u32[]{:S(2)}, u32[]{:S(2)}) %collective-permute-start.17) | collective-permute-done | bytes 163872 | tf_op jit(solution)/shard_map/ppermute | solution.py:320
  45.9 2.9 %collective-permute-start.11 = (bf16[64,1280]{1,0:T(8,128)(2,1)S(1)}, bf16[64,1280]{1,0:T(8,128)(2,1)S(1)}, u32[]{:S(2)}, u32[]{:S(2)}) collective-permute-start(bf16[64,1280]{1,0:T(8,128)(2,1)S(1)} %choose.4.refs_7_), channel_id=1, source_target_pairs={{0,4},{1,5},{2,6},{3,7},{4,0},{5,1},{6,2},{7,3},{8,12},{9,13},{10,... | collective-permute-start | bytes 491528 | tf_op jit(solution)/shard_map/ppermute | solution.py:320
  49.8 4.0 %collective-permute-done.3.refs_6_.refs_5_ = bf16[256,1280]{1,0:T(8,128)(2,1)S(1)} collective-permute-done((bf16[256,1280]{1,0:T(8,128)(2,1)S(1)}, bf16[256,1280]{1,0:T(8,128)(2,1)S(1)}, u32[]{:S(2)}, u32[]{:S(2)}) %collective-permute-start.3) | collective-permute-done | bytes 655392 | tf_op jit(solution)/shard_map/ppermute | solution.py:348
  53.8 3.5 %collective-permute-done.10.refs_8_ = bf16[64,1280]{1,0:T(8,128)(2,1)S(1)} collective-permute-done((bf16[64,1280]{1,0:T(8,128)(2,1)S(1)}, bf16[64,1280]{1,0:T(8,128)(2,1)S(1)}, u32[]{:S(2)}, u32[]{:S(2)}) %collective-permute-start.10) | collective-permute-done | bytes 163872 | tf_op jit(solution)/shard_map/ppermute | solution.py:320
  57.3 2.5 %collective-permute-start.19 = (bf16[64,1280]{1,0:T(8,128)(2,1)S(1)}, bf16[64,1280]{1,0:T(8,128)(2,1)S(1)}, u32[]{:S(2)}, u32[]{:S(2)}) collective-permute-start(bf16[64,1280]{1,0:T(8,128)(2,1)S(1)} %choose.5.refs_15_), channel_id=1, source_target_pairs={{0,4},{1,5},{2,6},{3,7},{4,0},{5,1},{6,2},{7,3},{8,12},{9,13},{10,... | collective-permute-start | bytes 491528 | tf_op jit(solution)/shard_map/ppermute | solution.py:320
  59.8 1.4 %collective-permute-start.20 = (bf16[64,1280]{1,0:T(8,128)(2,1)S(1)}, bf16[64,1280]{1,0:T(8,128)(2,1)S(1)}, u32[]{:S(2)}, u32[]{:S(2)}) collective-permute-start(bf16[64,1280]{1,0:T(8,128)(2,1)S(1)} %choose.5.refs_15_), channel_id=1, source_target_pairs={{0,6},{1,7},{2,4},{3,5},{4,2},{5,3},{6,0},{7,1},{8,14},{9,15},{10,... | collective-permute-start | bytes 491528 | tf_op jit(solution)/shard_map/ppermute | solution.py:320
  61.3 1.6 %collective-permute-done.12.refs_10_ = bf16[64,1280]{1,0:T(8,128)(2,1)S(1)} collective-permute-done((bf16[64,1280]{1,0:T(8,128)(2,1)S(1)}, bf16[64,1280]{1,0:T(8,128)(2,1)S(1)}, u32[]{:S(2)}, u32[]{:S(2)}) %collective-permute-start.12) | collective-permute-done | bytes 163872 | tf_op jit(solution)/shard_map/ppermute | solution.py:320
  62.9 1.5 %collective-permute-start.21 = (bf16[64,1280]{1,0:T(8,128)(2,1)S(1)}, bf16[64,1280]{1,0:T(8,128)(2,1)S(1)}, u32[]{:S(2)}, u32[]{:S(2)}) collective-permute-start(bf16[64,1280]{1,0:T(8,128)(2,1)S(1)} %choose.5.refs_15_), channel_id=1, source_target_pairs={{0,1},{1,0},{2,3},{3,2},{4,5},{5,4},{6,7},{7,6},{8,9},{9,8},{10,11... | collective-permute-start | bytes 491528 | tf_op jit(solution)/shard_map/ppermute | solution.py:320
  64.4 1.0 %attend.6 = bf16[1360,128]{1,0:T(8,128)(2,1)S(1)} custom-call(bf16[128,1408]{1,0:T(8,128)(2,1)S(1)} %collective-permute-done.4.refs_0_, bf16[128,2560]{1,0:T(8,128)(2,1)S(1)} %bitcast.15, bf16[128,2560]{1,0:T(8,128)(2,1)S(1)} %bitcast.22, bf16[128,2560]{1,0:T(8,128)(2,1)S(1)} %collective-permute-done.refs_4_.refs_3_, ...), custom_call_target="tpu_custom_call" | custom-call | flops 377487360 | bytes 3276800 | tf_op jit(solution)/shard_map/attend/pallas_call | solution.py:110
  66.4 1.9 %collective-permute-start.5 = (bf16[1360,128]{1,0:T(8,128)(2,1)S(1)}, bf16[1360,128]{1,0:T(8,128)(2,1)S(1)}, u32[]{:S(2)}, u32[]{:S(2)}) collective-permute-start(bf16[1360,128]{1,0:T(8,128)(2,1)S(1)} %attend.6), channel_id=1, source_target_pairs={{0,8},{8,16},{16,24},{1,9},{9,17},{17,25},{2,10},{10,18},{18,26},{... | collective-permute-start | bytes 1044488 | tf_op jit(solution)/shard_map/ppermute | solution.py:367
  68.3 1.9 %collective-permute-start.7 = (bf16[1360,128]{1,0:T(8,128)(2,1)S(1)}, bf16[1360,128]{1,0:T(8,128)(2,1)S(1)}, u32[]{:S(2)}, u32[]{:S(2)}) collective-permute-start(bf16[1360,128]{1,0:T(8,128)(2,1)S(1)} %attend.7), channel_id=1, source_target_pairs={{0,8},{8,16},{16,24},{1,9},{9,17},{17,25},{2,10},{10,18},{18,26},{... | collective-permute-start | bytes 1044488 | tf_op jit(solution)/shard_map/ppermute | solution.py:367
  74.4 4.9 %collective-permute-done.5.refs_5_ = bf16[1360,128]{1,0:T(8,128)(2,1)S(1)} collective-permute-done((bf16[1360,128]{1,0:T(8,128)(2,1)S(1)}, bf16[1360,128]{1,0:T(8,128)(2,1)S(1)}, u32[]{:S(2)}, u32[]{:S(2)}) %collective-permute-start.5) | collective-permute-done | bytes 348192 | tf_op jit(solution)/shard_map/ppermute | solution.py:367
  79.3 6.5 %collective-permute-done.7.refs_6_ = bf16[1360,128]{1,0:T(8,128)(2,1)S(1)} collective-permute-done((bf16[1360,128]{1,0:T(8,128)(2,1)S(1)}, bf16[1360,128]{1,0:T(8,128)(2,1)S(1)}, u32[]{:S(2)}, u32[]{:S(2)}) %collective-permute-start.7) | collective-permute-done | bytes 348192 | tf_op jit(solution)/shard_map/ppermute | solution.py:367
  85.8 2.4 %final.1 = bf16[128,2560]{1,0:T(8,128)(2,1)} custom-call(bf16[128,2560]{1,0:T(8,128)(2,1)S(1)} %bitcast.29, f32[1280,128]{1,0:T(8,128)S(1)} %get-tuple-element.19.refs_1_, f32[1280,128]{1,0:T(8,128)S(1)} %get-tuple-element.21.refs_2_, f32[32,128]{1,0:T(8,128)S(1)} %get-tuple-element.22.refs_3_, f32[32,128]{1,0:T(8,128)S(1)} %get-tuple-element.23.refs_4_, ...), custom_call_target="tpu_custom_call" | custom-call | flops 503316480 | bytes 5242880 | tf_op jit(solution)/shard_map/final/pallas_call | solution.py:177
  (45 shorter events, 9.9 us)
Async XLA Ops:
  3.3 22.2 %collective-permute-start.4 = (bf16[128,1408]{1,0:T(8,128)(2,1)S(1)}, bf16[128,1408]{1,0:T(8,128)(2,1)S(1)}, u32[]{:S(2)}, u32[]{:S(2)}) collective-permute-start(bf16[128,1408]{1,0:T(8,128)(2,1)S(1)} %get-tuple-element.24), channel_id=1, source_target_pairs={{8,0},{16,8},{24,16},{9,1},{17,9},{25,17},{10,2},{18,10},{26,18},{... | collective-permute-start | bytes 1081352 | tf_op jit(solution)/shard_map/ppermute | solution.py:350
  7.6 16.0 %collective-permute-start.8 = (bf16[64,2560]{1,0:T(8,128)(2,1)S(1)}, bf16[64,2560]{1,0:T(8,128)(2,1)S(1)}, u32[]{:S(2)}, u32[]{:S(2)}) collective-permute-start(bf16[64,2560]{1,0:T(8,128)(2,1)S(1)} %get-tuple-element.26.x), channel_id=1, source_target_pairs={{0,8},{8,0},{16,24},{24,16},{1,9},{9,1},{17,25},{25,17},{2,10},{10... | collective-permute-start | bytes 983048 | tf_op jit(solution)/shard_map/ppermute | solution.py:320
  9.3 21.0 %collective-permute-start.6 = (bf16[128,1408]{1,0:T(8,128)(2,1)S(1)}, bf16[128,1408]{1,0:T(8,128)(2,1)S(1)}, u32[]{:S(2)}, u32[]{:S(2)}) collective-permute-start(bf16[128,1408]{1,0:T(8,128)(2,1)S(1)} %get-tuple-element.25), channel_id=1, source_target_pairs={{8,0},{16,8},{24,16},{9,1},{17,9},{25,17},{10,2},{18,10},{26,18},{... | collective-permute-start | bytes 1081352 | tf_op jit(solution)/shard_map/ppermute | solution.py:350
  11.2 34.6 %collective-permute-start = (bf16[128,2560]{1,0:T(8,128)(2,1)S(1)}, bf16[128,2560]{1,0:T(8,128)(2,1)S(1)}, u32[]{:S(2)}, u32[]{:S(2)}) collective-permute-start(bf16[128,2560]{1,0:T(8,128)(2,1)S(1)} %bitcast.14), channel_id=1, source_target_pairs={{0,1},{1,0},{2,3},{3,2},{4,5},{5,4},{6,7},{7,6},{8,9},{9,8},{10,11... | collective-permute-start | bytes 1966088 | tf_op jit(solution)/shard_map/ppermute | solution.py:320
  11.3 37.4 %collective-permute-start.1 = (bf16[128,2560]{1,0:T(8,128)(2,1)S(1)}, bf16[128,2560]{1,0:T(8,128)(2,1)S(1)}, u32[]{:S(2)}, u32[]{:S(2)}) collective-permute-start(bf16[128,2560]{1,0:T(8,128)(2,1)S(1)} %bitcast.21), channel_id=1, source_target_pairs={{0,1},{1,0},{2,3},{3,2},{4,5},{5,4},{6,7},{7,6},{8,9},{9,8},{10,11... | collective-permute-start | bytes 1966088 | tf_op jit(solution)/shard_map/ppermute | solution.py:320
  23.7 26.1 %collective-permute-start.2 = (bf16[256,1280]{1,0:T(8,128)(2,1)S(1)}, bf16[256,1280]{1,0:T(8,128)(2,1)S(1)}, u32[]{:S(2)}, u32[]{:S(2)}) collective-permute-start(bf16[256,1280]{1,0:T(8,128)(2,1)S(1)} %get-tuple-element.18), channel_id=1, source_target_pairs={{1,2},{3,4},{5,6},{2,1},{4,3},{6,5},{9,10},{11,12},{13,14},{10,9},... | collective-permute-start | bytes 1966088 | tf_op jit(solution)/shard_map/ppermute | solution.py:348
  25.6 28.2 %collective-permute-start.3 = (bf16[256,1280]{1,0:T(8,128)(2,1)S(1)}, bf16[256,1280]{1,0:T(8,128)(2,1)S(1)}, u32[]{:S(2)}, u32[]{:S(2)}) collective-permute-start(bf16[256,1280]{1,0:T(8,128)(2,1)S(1)} %get-tuple-element.20), channel_id=1, source_target_pairs={{1,2},{3,4},{5,6},{2,1},{4,3},{6,5},{9,10},{11,12},{13,14},{10,9},... | collective-permute-start | bytes 1966088 | tf_op jit(solution)/shard_map/ppermute | solution.py:348
  30.3 6.6 %collective-permute-start.9 = (bf16[64,1280]{1,0:T(8,128)(2,1)S(1)}, bf16[64,1280]{1,0:T(8,128)(2,1)S(1)}, u32[]{:S(2)}, u32[]{:S(2)}) collective-permute-start(bf16[64,1280]{1,0:T(8,128)(2,1)S(1)} %get-tuple-element.27.x), channel_id=1, source_target_pairs={{0,16},{8,24},{16,0},{24,8},{1,17},{9,25},{17,1},{25,9},{2,18},{10... | collective-permute-start | bytes 491528 | tf_op jit(solution)/shard_map/ppermute | solution.py:320
  36.9 8.5 %collective-permute-start.17 = (bf16[64,1280]{1,0:T(8,128)(2,1)S(1)}, bf16[64,1280]{1,0:T(8,128)(2,1)S(1)}, u32[]{:S(2)}, u32[]{:S(2)}) collective-permute-start(bf16[64,1280]{1,0:T(8,128)(2,1)S(1)} %get-tuple-element.28.x), channel_id=1, source_target_pairs={{0,16},{8,24},{16,0},{24,8},{1,17},{9,25},{17,1},{25,9},{2,18},{10... | collective-permute-start | bytes 491528 | tf_op jit(solution)/shard_map/ppermute | solution.py:320
  45.3 12.0 %collective-permute-start.10 = (bf16[64,1280]{1,0:T(8,128)(2,1)S(1)}, bf16[64,1280]{1,0:T(8,128)(2,1)S(1)}, u32[]{:S(2)}, u32[]{:S(2)}) collective-permute-start(bf16[64,1280]{1,0:T(8,128)(2,1)S(1)} %choose.4.refs_7_), channel_id=1, source_target_pairs={{0,2},{1,3},{2,0},{3,1},{4,6},{5,7},{6,4},{7,5},{8,10},{9,11},{10,... | collective-permute-start | bytes 491528 | tf_op jit(solution)/shard_map/ppermute | solution.py:320
  45.9 14.0 %collective-permute-start.11 = (bf16[64,1280]{1,0:T(8,128)(2,1)S(1)}, bf16[64,1280]{1,0:T(8,128)(2,1)S(1)}, u32[]{:S(2)}, u32[]{:S(2)}) collective-permute-start(bf16[64,1280]{1,0:T(8,128)(2,1)S(1)} %choose.4.refs_7_), channel_id=1, source_target_pairs={{0,4},{1,5},{2,6},{3,7},{4,0},{5,1},{6,2},{7,3},{8,12},{9,13},{10,... | collective-permute-start | bytes 491528 | tf_op jit(solution)/shard_map/ppermute | solution.py:320
  48.7 14.1 %collective-permute-start.12 = (bf16[64,1280]{1,0:T(8,128)(2,1)S(1)}, bf16[64,1280]{1,0:T(8,128)(2,1)S(1)}, u32[]{:S(2)}, u32[]{:S(2)}) collective-permute-start(bf16[64,1280]{1,0:T(8,128)(2,1)S(1)} %choose.4.refs_7_), channel_id=1, source_target_pairs={{0,6},{1,7},{2,4},{3,5},{4,2},{5,3},{6,0},{7,1},{8,14},{9,15},{10,... | collective-permute-start | bytes 491528 | tf_op jit(solution)/shard_map/ppermute | solution.py:320
  49.7 16.7 %collective-permute-start.13 = (bf16[64,1280]{1,0:T(8,128)(2,1)S(1)}, bf16[64,1280]{1,0:T(8,128)(2,1)S(1)}, u32[]{:S(2)}, u32[]{:S(2)}) collective-permute-start(bf16[64,1280]{1,0:T(8,128)(2,1)S(1)} %choose.4.refs_7_), channel_id=1, source_target_pairs={{0,1},{1,0},{2,3},{3,2},{4,5},{5,4},{6,7},{7,6},{8,9},{9,8},{10,11... | collective-permute-start | bytes 491528 | tf_op jit(solution)/shard_map/ppermute | solution.py:320
  53.8 14.5 %collective-permute-start.18 = (bf16[64,1280]{1,0:T(8,128)(2,1)S(1)}, bf16[64,1280]{1,0:T(8,128)(2,1)S(1)}, u32[]{:S(2)}, u32[]{:S(2)}) collective-permute-start(bf16[64,1280]{1,0:T(8,128)(2,1)S(1)} %choose.5.refs_15_), channel_id=1, source_target_pairs={{0,2},{1,3},{2,0},{3,1},{4,6},{5,7},{6,4},{7,5},{8,10},{9,11},{10,... | collective-permute-start | bytes 491528 | tf_op jit(solution)/shard_map/ppermute | solution.py:320
  57.3 12.9 %collective-permute-start.19 = (bf16[64,1280]{1,0:T(8,128)(2,1)S(1)}, bf16[64,1280]{1,0:T(8,128)(2,1)S(1)}, u32[]{:S(2)}, u32[]{:S(2)}) collective-permute-start(bf16[64,1280]{1,0:T(8,128)(2,1)S(1)} %choose.5.refs_15_), channel_id=1, source_target_pairs={{0,4},{1,5},{2,6},{3,7},{4,0},{5,1},{6,2},{7,3},{8,12},{9,13},{10,... | collective-permute-start | bytes 491528 | tf_op jit(solution)/shard_map/ppermute | solution.py:320
  59.8 10.5 %collective-permute-start.20 = (bf16[64,1280]{1,0:T(8,128)(2,1)S(1)}, bf16[64,1280]{1,0:T(8,128)(2,1)S(1)}, u32[]{:S(2)}, u32[]{:S(2)}) collective-permute-start(bf16[64,1280]{1,0:T(8,128)(2,1)S(1)} %choose.5.refs_15_), channel_id=1, source_target_pairs={{0,6},{1,7},{2,4},{3,5},{4,2},{5,3},{6,0},{7,1},{8,14},{9,15},{10,... | collective-permute-start | bytes 491528 | tf_op jit(solution)/shard_map/ppermute | solution.py:320
  62.9 8.0 %collective-permute-start.21 = (bf16[64,1280]{1,0:T(8,128)(2,1)S(1)}, bf16[64,1280]{1,0:T(8,128)(2,1)S(1)}, u32[]{:S(2)}, u32[]{:S(2)}) collective-permute-start(bf16[64,1280]{1,0:T(8,128)(2,1)S(1)} %choose.5.refs_15_), channel_id=1, source_target_pairs={{0,1},{1,0},{2,3},{3,2},{4,5},{5,4},{6,7},{7,6},{8,9},{9,8},{10,11... | collective-permute-start | bytes 491528 | tf_op jit(solution)/shard_map/ppermute | solution.py:320
  66.4 12.9 %collective-permute-start.5 = (bf16[1360,128]{1,0:T(8,128)(2,1)S(1)}, bf16[1360,128]{1,0:T(8,128)(2,1)S(1)}, u32[]{:S(2)}, u32[]{:S(2)}) collective-permute-start(bf16[1360,128]{1,0:T(8,128)(2,1)S(1)} %attend.6), channel_id=1, source_target_pairs={{0,8},{8,16},{16,24},{1,9},{9,17},{17,25},{2,10},{10,18},{18,26},{... | collective-permute-start | bytes 1044488 | tf_op jit(solution)/shard_map/ppermute | solution.py:367
  68.3 17.5 %collective-permute-start.7 = (bf16[1360,128]{1,0:T(8,128)(2,1)S(1)}, bf16[1360,128]{1,0:T(8,128)(2,1)S(1)}, u32[]{:S(2)}, u32[]{:S(2)}) collective-permute-start(bf16[1360,128]{1,0:T(8,128)(2,1)S(1)} %attend.7), channel_id=1, source_target_pairs={{0,8},{8,16},{16,24},{1,9},{9,17},{17,25},{2,10},{10,18},{18,26},{... | collective-permute-start | bytes 1044488 | tf_op jit(solution)/shard_map/ppermute | solution.py:367
  70.3 1.5 %collective-permute-start.14 = (bf16[64,1280]{1,0:T(8,128)(2,1)S(1)}, bf16[64,1280]{1,0:T(8,128)(2,1)S(1)}, u32[]{:S(2)}, u32[]{:S(2)}) collective-permute-start(bf16[64,1280]{1,0:T(8,128)(2,1)S(1)} %collective-permute-done.10.refs_8_), channel_id=1, source_target_pairs={{0,1},{1,0},{2,3},{3,2},{4,5},{5,4},{6,7},{7,6},{8,9},{9,8},{10,11... | collective-permute-start | bytes 491528 | tf_op jit(solution)/shard_map/ppermute | solution.py:320
  70.4 1.6 %collective-permute-start.15 = (bf16[64,1280]{1,0:T(8,128)(2,1)S(1)}, bf16[64,1280]{1,0:T(8,128)(2,1)S(1)}, u32[]{:S(2)}, u32[]{:S(2)}) collective-permute-start(bf16[64,1280]{1,0:T(8,128)(2,1)S(1)} %collective-permute-done.11.refs_9_), channel_id=1, source_target_pairs={{0,1},{1,0},{2,3},{3,2},{4,5},{5,4},{6,7},{7,6},{8,9},{9,8},{10,11... | collective-permute-start | bytes 491528 | tf_op jit(solution)/shard_map/ppermute | solution.py:320
  71.7 2.7 %collective-permute-start.22 = (bf16[64,1280]{1,0:T(8,128)(2,1)S(1)}, bf16[64,1280]{1,0:T(8,128)(2,1)S(1)}, u32[]{:S(2)}, u32[]{:S(2)}) collective-permute-start(bf16[64,1280]{1,0:T(8,128)(2,1)S(1)} %collective-permute-done.18.refs_16_), channel_id=1, source_target_pairs={{0,1},{1,0},{2,3},{3,2},{4,5},{5,4},{6,7},{7,6},{8,9},{9,8},{10,11... | collective-permute-start | bytes 491528 | tf_op jit(solution)/shard_map/ppermute | solution.py:320
  72.0 2.5 %collective-permute-start.23 = (bf16[64,1280]{1,0:T(8,128)(2,1)S(1)}, bf16[64,1280]{1,0:T(8,128)(2,1)S(1)}, u32[]{:S(2)}, u32[]{:S(2)}) collective-permute-start(bf16[64,1280]{1,0:T(8,128)(2,1)S(1)} %collective-permute-done.19.refs_17_), channel_id=1, source_target_pairs={{0,1},{1,0},{2,3},{3,2},{4,5},{5,4},{6,7},{7,6},{8,9},{9,8},{10,11... | collective-permute-start | bytes 491528 | tf_op jit(solution)/shard_map/ppermute | solution.py:320
  72.2 2.2 %collective-permute-start.24 = (bf16[64,1280]{1,0:T(8,128)(2,1)S(1)}, bf16[64,1280]{1,0:T(8,128)(2,1)S(1)}, u32[]{:S(2)}, u32[]{:S(2)}) collective-permute-start(bf16[64,1280]{1,0:T(8,128)(2,1)S(1)} %collective-permute-done.20.refs_18_), channel_id=1, source_target_pairs={{0,1},{1,0},{2,3},{3,2},{4,5},{5,4},{6,7},{7,6},{8,9},{9,8},{10,11... | collective-permute-start | bytes 491528 | tf_op jit(solution)/shard_map/ppermute | solution.py:320
  (5 other events, 25.1 us)
